TPU v7x, 768 devices: a whole 4x8x12 slice. The times are simulated.
768 devices in a mesh: height: 96 (over y, z_lo, core), dp: 8 (over z_hi, x).
Axes of the slice: x: 4, y: 8, z: 12 (z_hi: 2, z_lo: 6; z = z_hi * 6 + z_lo), core: 2. Of those that a mesh axis runs over, the one named last changes fastest.
Arguments:
- x_next: bfloat16 [8, 192, 320, 128], P('dp', 'height'), may hold values from -12 to 12
- x_cur: bfloat16 [8, 192, 320, 128], P('dp', 'height'), may hold values from -12 to 12
- grad_out: bfloat16 [8, 192, 320, 128], P('dp', 'height'), may hold values from -6 to 6
- kernel: bfloat16 [3, 3, 320, 320], replicated, may hold values from -0.109375 to 0.109375
- gamma: float32 [320], replicated, may hold values from 0.25 to 1.75
- beta: float32 [320], replicated, may hold values from -2.5 to 2.5
Outputs:
- y_next: bfloat16 [8, 192, 320, 128], P('dp', 'height')
- grad_x: bfloat16 [8, 192, 320, 128], P('dp', 'height')
- grad_kernel: float32 [921600], P(('height', 'dp'))
All inputs are finite; a program needn't handle non-finite values.
Results may differ from a plain program's by a relative error of at most 0.0049.
Values may be sent and summed in bfloat16 or wider, within the bound.
A program may use at most 64 MiB of HBM per device.

v0:
```python
import jax
import jax.numpy as jnp
from jax import lax
from jax.sharding import Mesh
from jax.sharding import PartitionSpec as P

CHANNELS = 320
GROUPS = 32
HEIGHT = ("height_0", "height_1", "height_2")
HEIGHT_DP = ("height_0", "height_1", "height_2", "dp")


eps = 1e-05


def extended(cells, sides, width):
    for axis, dim in sides:
        count = lax.axis_size(axis)
        ends = count - 1
        head = lax.slice_in_dim(cells, 0, width, axis=dim)
        tail = lax.slice_in_dim(cells, cells.shape[dim] - width, cells.shape[dim], axis=dim)
        cells = jnp.concatenate(
            [
                lax.ppermute(tail, axis, [(i, (i + 1) % count) for i in range(ends)]),
                cells,
                lax.ppermute(head, axis, [((i + 1) % count, i) for i in range(ends)]),
            ],
            axis=dim,
        )
    return cells


def one_axis_at_a_time(value, axes):
    for axis in axes:
        value = lax.psum(value, axis)
    return value


def conv_rows(padded, kernel, count):
    width = padded.shape[-1]
    wide = jnp.pad(padded, ((0, 0), (0, 0), (0, 0), (1, 1)))
    total = None
    for tap_row in range(3):
        for tap_col in range(3):
            window = wide[:, tap_row : tap_row + count, :, tap_col : tap_col + width]
            term = jnp.einsum(
                "oc,bhcw->bhow",
                kernel[tap_row, tap_col],
                window,
                preferred_element_type=jnp.float32,
            )
            total = term if total is None else total + term
    return total


def group_sum(value):
    batch, rows, chans, width = value.shape
    return jnp.sum(value.reshape(batch, rows, GROUPS, chans // GROUPS, width), axis=(1, 3, 4))


def expand(stat):
    return jnp.repeat(stat, CHANNELS // GROUPS, axis=1)[:, None, :, None]


def local(x_next, x_cur, grad_out, kernel, gamma, beta):
    batch, rows, chans, width = x_next.shape
    height_count = lax.axis_size(HEIGHT)
    count = height_count * rows * (CHANNELS // GROUPS) * width
    gain = gamma[None, None, :, None]
    shift_b = beta[None, None, :, None]
    stacked = jnp.stack((x_next, x_cur, grad_out))
    padded = extended(stacked, ((HEIGHT, 2),), 2)
    xp_next = padded[0, :, 1:-1]
    xp_cur = padded[1]
    grad_rows = padded[2, :, 1:-1]
    offset_rows = 1
    z_next = conv_rows(xp_next, kernel, rows)
    z_back = conv_rows(xp_cur, kernel, rows + 2)
    z_cur = z_back[:, 1:-1]
    sum_next, sum_cur, sq_next, sq_cur = (
        one_axis_at_a_time(group_sum(z_next), HEIGHT),
        one_axis_at_a_time(group_sum(z_cur), HEIGHT),
        one_axis_at_a_time(group_sum(z_next * z_next), HEIGHT),
        one_axis_at_a_time(group_sum(z_cur * z_cur), HEIGHT),
    )
    mean_next = sum_next / count
    mean_cur = sum_cur / count
    var_next = sq_next / count - mean_next * mean_next
    var_cur = sq_cur / count - mean_cur * mean_cur
    rstd_next = lax.rsqrt(var_next + eps)
    rstd_cur = lax.rsqrt(var_cur + eps)
    affine_next = (z_next - expand(mean_next)) * expand(rstd_next) * gain + shift_b
    y_next = (affine_next * jax.nn.sigmoid(affine_next)).astype(jnp.bfloat16)
    normed = (z_back - expand(mean_cur)) * expand(rstd_cur)
    affine = normed * gain + shift_b
    sig = jax.nn.sigmoid(affine)
    grad_n = grad_rows.astype(jnp.float32) * (sig * (1.0 + affine * (1.0 - sig))) * gain
    last_row = offset_rows + rows
    gn_own = grad_n[:, offset_rows:last_row]
    n_own = normed[:, offset_rows:last_row]
    first_sum, second_sum = (
        one_axis_at_a_time(group_sum(gn_own), HEIGHT),
        one_axis_at_a_time(group_sum(gn_own * n_own), HEIGHT),
    )
    grad_z = (
        expand(rstd_cur)
        * (grad_n - expand(first_sum / count) - normed * expand(second_sum / count))
    ).astype(jnp.bfloat16)
    position = lax.axis_index(HEIGHT)
    row_ids = jnp.arange(rows + 2)
    outside = (row_ids == 0) & (position == 0) | (row_ids == rows + 1) & (
        position == height_count - 1
    )
    grad_pad = jnp.where(outside[None, :, None, None], jnp.zeros_like(grad_z), grad_z)
    grad_own = grad_pad[:, 1:-1]
    grad_wide = jnp.pad(grad_pad, ((0, 0), (0, 0), (0, 0), (1, 1)))
    x_wide = jnp.pad(xp_cur, ((0, 0), (0, 0), (0, 0), (1, 1)))
    grad_input = None
    taps = []
    for tap_row in range(3):
        tap_list = []
        for tap_col in range(3):
            window = grad_wide[
                :, 2 - tap_row : 2 - tap_row + rows, :, 2 - tap_col : 2 - tap_col + width
            ]
            term = jnp.einsum(
                "oc,bhow->bhcw",
                kernel[tap_row, tap_col],
                window,
                preferred_element_type=jnp.float32,
            )
            grad_input = term if grad_input is None else grad_input + term
            start = tap_row + offset_rows
            source = x_wide[:, start : start + rows, :, tap_col : tap_col + width]
            tap_list.append(
                jnp.einsum("bhow,bhcw->oc", grad_own, source, preferred_element_type=jnp.float32)
            )
        taps.append(jnp.stack(tap_list))
    grad_local = jnp.stack(taps)
    grad_x = grad_input.astype(jnp.bfloat16)
    group_count = lax.axis_size("dp")
    piece = grad_local.size // (height_count * group_count)
    flat = grad_local.reshape(height_count * group_count * piece)
    grad_kernel = lax.psum_scatter(flat, HEIGHT_DP, scatter_dimension=0, tiled=True)
    return (y_next, grad_x, grad_kernel)


def solution(mesh):
    torus = Mesh(
        mesh.devices.reshape(8, 6, 2, mesh.shape["dp"]), ("height_0", "height_1", "height_2", "dp")
    )
    in_specs = (
        P("dp", HEIGHT, None, None),
        P("dp", HEIGHT, None, None),
        P("dp", HEIGHT, None, None),
        P(),
        P(),
        P(),
    )
    out_specs = (P("dp", HEIGHT, None, None), P("dp", HEIGHT, None, None), P(HEIGHT_DP))
    return jax.shard_map(local, mesh=torus, in_specs=in_specs, out_specs=out_specs, check_vma=False)
```

profile of v0, /device:TPU:24, one launch (start us, length us, event | category | flops | bytes accessed | tf_op | source)
XLA Modules:
  0.0 655.0 jit_solution(2714242735615253450)
XLA Ops:
  7.2 2.0 pad_maximum_fusion.1
  9.3 12.0 %collective-permute-start.1 = (bf16[3,1,2,320,128]{4,3,2,1,0:T(8,128)(2,1)}, bf16[3,1,2,320,128]{4,3,2,1,0:T(8,128)(2,1)S(1)}, u32[]{:S(2)}, u32[]{:S(2)}) collective-permute-start(bf16[3,1,2,320,128]{4,3,2,1,0:T(8,128)(2,1)} %pad_maximum_fusion.1), channel_id=1, source_target_pairs={{8,0},{16,8},{24,16},{32,24},{40,32},{48,40},{56,48},{64,56},{72,6... | collective-permute-start | bytes 1474568 | tf_op jit(solution)/shard_map/ppermute | solution.py:26
  21.3 1.9 collective-permute-start
  23.3 0.5 and_or_fusion
  23.8 4.2 collective-permute-done.1
  28.0 9.4 %collective-permute-done = bf16[3,1,2,320,128]{4,3,2,1,0:T(8,128)(2,1)S(1)} collective-permute-done((bf16[3,1,2,320,128]{4,3,2,1,0:T(8,128)(2,1)}, bf16[3,1,2,320,128]{4,3,2,1,0:T(8,128)(2,1)S(1)}, u32[]{:S(2)}, u32[]{:S(2)}) %collective-permute-start) | collective-permute-done | bytes 491552 | tf_op jit(solution)/shard_map/ppermute | solution.py:24
  37.4 1.1 maximum_bitcast_fusion.4
  40.9 0.4 fusion.23
  41.5 0.6 reduce_sum.87
  42.4 0.6 reduce_sum.80
  43.0 1.1 maximum_bitcast_fusion.3
  44.1 0.4 fusion.6
  44.8 0.4 convolution_add_fusion.6
  45.3 0.4 convolution_add_fusion.5
  46.1 0.4 convolution_add_fusion.3
  46.5 0.4 convolution_add_fusion.2
  47.3 0.4 fusion
  47.8 0.8 copy-done.4
  49.2 16.9 %all-reduce.5 = (f32[1,32]{1,0:T(1,128)S(1)}, f32[1,32]{1,0:T(1,128)S(1)}) all-reduce(f32[1,32]{1,0:T(1,128)S(1)} %bitcast.337, f32[1,32]{1,0:T(1,128)S(1)} %bitcast.338), channel_id=1, replica_groups=mesh['height_0'=8,'height_1'=6,'height_2'=2,'dp'=8] {'height_0'}, use_global_device_ids=true, to_apply=%region_17.18 | all-reduce | flops 64 | bytes 512 | tf_op jit(solution)/shard_map/psum | solution.py:35
  66.2 19.8 %all-reduce.7 = (f32[1,32]{1,0:T(1,128)S(1)}, f32[1,32]{1,0:T(1,128)S(1)}) all-reduce(f32[1,32]{1,0:T(1,128)S(1)} %get-tuple-element.11, f32[1,32]{1,0:T(1,128)S(1)} %get-tuple-element.12), channel_id=1, replica_groups=mesh['height_0'=8,'height_1'=6,'height_2'=2,'dp'=8] {'height_1'}, use_global_device_ids=true, to_apply=%region_18.19 | all-reduce | flops 64 | bytes 512 | tf_op jit(solution)/shard_map/psum | solution.py:35
  86.0 2.5 all-reduce.9
  88.8 1.6 fusion.3
  90.5 0.8 copy-done.2
  92.0 14.7 %all-reduce.4 = (f32[1,32]{1,0:T(1,128)S(1)}, f32[1,32]{1,0:T(1,128)S(1)}, f32[1,32]{1,0:T(1,128)S(1)}, f32[1,32]{1,0:T(1,128)S(1)}) all-reduce(f32[1,32]{1,0:T(1,128)} %bitcast.333, f32[1,32]{1,0:T(1,128)} %bitcast.334, f32[1,32]{1,0:T(1,128)S(1)} %bitcast.335, ...), channel_id=1, replica_groups=mesh['height_0'=8,'height_1'=6,'height_2'=2,'dp'=8] {'height_0'}, use_global_device_ids=true, to_apply=%region_7.8 | all-reduce | flops 128 | bytes 1024 | tf_op jit(solution)/shard_map/psum | solution.py:35
  106.7 19.8 %all-reduce.6 = (f32[1,32]{1,0:T(1,128)S(1)}, f32[1,32]{1,0:T(1,128)S(1)}, f32[1,32]{1,0:T(1,128)S(1)}, f32[1,32]{1,0:T(1,128)S(1)}) all-reduce(f32[1,32]{1,0:T(1,128)S(1)} %get-tuple-element.7, f32[1,32]{1,0:T(1,128)S(1)} %get-tuple-element.8, ...), channel_id=1, replica_groups=mesh['height_0'=8,'height_1'=6,'height_2'=2,'dp'=8] {'height_1'}, use_global_device_ids=true, to_apply=%region_8.9 | all-reduce | flops 128 | bytes 1024 | tf_op jit(solution)/shard_map/psum | solution.py:35
  126.5 2.6 all-reduce.8
  129.5 1.5 fusion.4
  131.0 1.1 fusion.52
  132.1 1.1 convolution_bitcast_fusion
  133.2 1.1 convolution_bitcast_fusion.1
  134.3 1.1 convolution_bitcast_fusion.2
  135.4 1.1 convolution_bitcast_fusion.3
  136.5 1.1 convolution_bitcast_fusion.4
  137.6 1.1 convolution_bitcast_fusion.5
  138.7 1.1 convolution_bitcast_fusion.6
  139.9 1.1 convolution_bitcast_fusion.7
  140.9 1.1 convolution_bitcast_fusion.8
  142.5 2.1 convolution_add_fusion.23
  144.6 1.4 maximum_bitcast_fusion.2
  146.2 0.9 copy-done.5
  147.5 2.3 pad_maximum_fusion
  149.8 5.7 reshape.287
  155.5 0.9 copy-done.11
  156.8 0.4 convolution_add_fusion.21
  158.5 1.0 fusion.2
  159.5 0.9 fusion.27
  160.4 486.3 %all-reduce.12.cloned.1.call-done = f32[921600]{0:T(1024)} async-done(((f32[921600]{0:T(1024)}), f32[921600]{0:T(1024)}) %all-reduce.12.cloned.1.call-update) | async-done | bytes 3686416
  646.7 1.4 dynamic-slice
  (72 shorter events, 8.3 us)
Async XLA Ops:
  7.2 31.4 %copy-start = (bf16[3,3,320,320]{3,2,1,0:T(8,128)(2,1)S(1)}, bf16[3,3,320,320]{3,2,1,0:T(8,128)(2,1)}, u32[]{:S(2)}) copy-start(bf16[3,3,320,320]{3,2,1,0:T(8,128)(2,1)} %param.9) | copy-start | bytes 5529604
  7.2 639.6 %all-reduce.12.cloned.1.call-start = ((), (), s32[]{:S(2)}) async-start(), calls=%async_computation | async-start | bytes 7372800
  9.3 18.7 %collective-permute-start.1 = (bf16[3,1,2,320,128]{4,3,2,1,0:T(8,128)(2,1)}, bf16[3,1,2,320,128]{4,3,2,1,0:T(8,128)(2,1)S(1)}, u32[]{:S(2)}, u32[]{:S(2)}) collective-permute-start(bf16[3,1,2,320,128]{4,3,2,1,0:T(8,128)(2,1)} %pad_maximum_fusion.1), channel_id=1, source_target_pairs={{8,0},{16,8},{24,16},{32,24},{40,32},{48,40},{56,48},{64,56},{72,6... | collective-permute-start | bytes 1474568 | tf_op jit(solution)/shard_map/ppermute | solution.py:26
  21.3 16.1 %collective-permute-start = (bf16[3,1,2,320,128]{4,3,2,1,0:T(8,128)(2,1)}, bf16[3,1,2,320,128]{4,3,2,1,0:T(8,128)(2,1)S(1)}, u32[]{:S(2)}, u32[]{:S(2)}) collective-permute-start(bf16[3,1,2,320,128]{4,3,2,1,0:T(8,128)(2,1)} %pad_maximum_fusion.1), channel_id=1, source_target_pairs={{0,8},{8,16},{16,24},{24,32},{32,40},{40,48},{48,56},{56,64},{64,7... | collective-permute-start | bytes 1474568 | tf_op jit(solution)/shard_map/ppermute | solution.py:24
  37.4 2.1 copy-start.1
  47.0 41.9 %copy-start.12 = (f32[320]{0:T(512)S(1)}, f32[320]{0:T(512)}, u32[]{:S(2)}) copy-start(f32[320]{0:T(512)} %param.11) | copy-start | bytes 3844
  47.0 41.9 %copy-start.13 = (f32[320]{0:T(512)S(1)}, f32[320]{0:T(512)}, u32[]{:S(2)}) copy-start(f32[320]{0:T(512)} %param.10) | copy-start | bytes 3844
  47.8 0.8 copy-start.4
  90.5 0.9 copy-start.2
  90.5 1.1 copy-start.3
  142.1 3.9 copy-start.8
  142.4 3.6 copy-start.9
  142.5 3.6 copy-start.10
  146.0 1.0 copy-start.5
  146.0 1.2 copy-start.6
  146.0 1.3 copy-start.7
  155.4 1.0 copy-start.11
Sparse Core Ops, SparseCore 0:
  155.6 491.0 all-reduce.11
where the time goes:
time: 656 us; the launch traced here: 655 us
  waiting for transfers between devices  500 us (76%)
  blocking collectives  76.3 us (12%)
  matrix products  22.6 us (3%)
  other arithmetic  15 us (2%)
  between operations  14.5 us (2%)
  starting transfers between devices  14 us (2%)
  local copies, waits for them, and re-layouts  12.6 us (2%)
    unnamed x2, waiting for transfers between devices  486 us
    psum x6, blocking collectives, one_axis_at_a_time(): value = lax.psum(value, axis)  76.3 us
  transfers between devices with their start and end apart: 3, of which 3 were waited for; matrix products, arithmetic and copies ran while one was open for 1% of the time, Pallas kernels for 0%

commit v1 on v0

v1 whole, which is shorter than its diff:
```python
import jax
import jax.numpy as jnp
from jax import lax
from jax.experimental import pallas as pl
from jax.experimental.pallas import tpu as pltpu
from jax.sharding import Mesh
from jax.sharding import PartitionSpec as P

CH = 320
COLS = 128
PAD = 384
GROUP = 10
NY, NZL, NC, NZH, NX = 8, 6, 2, 2, 4
NM = NZL * NC
NH = NY * NM
NZ = NZL * NZH
COUNT = 192 * GROUP * COLS
EPS = 1e-05
HEIGHT = ("y", "zl", "core")
DP = ("zh", "x")
FIRST = (0, 10, 21)
BLOCKS = (11, 12, 11)
ORDER = (0, 3, 1, 4, 2, 5)

f32 = jnp.float32
bf16 = jnp.bfloat16


def dot(a, b, dims=(((1,), (0,)), ((), ()))):
    return lax.dot_general(a, b, dims, preferred_element_type=f32)


NT = (((1,), (1,)), ((), ()))
TN = (((0,), (0,)), ((), ()))


def body(
    xn_in, xc_in, go_in, k_in, gam_in, bet_in,
    y_out, gx_out, gk_out,
    xcr, xnr, gor, kv, xcs, xns, gzo, gzh, gzs,
    zc, zn, nrm, gn, emask, gam, bet, selm,
    ra, rb, ra2, rb2,
    gacc, s1, r1, s2, r2, s3, r3, s4, r4, bown, s5, cown, r5, r6,
    lsem, hs, hr, ghs, ghr, as_, ar, bs, br, as2, ar2, bs2, br2,
    c1s, c1r, c2s, c2r, c3s, c3r, c4s, c4r, c5s, c5r, c6s, c6r,
):
    yy, zl, co = lax.axis_index("y"), lax.axis_index("zl"), lax.axis_index("core")
    zh, xx = lax.axis_index("zh"), lax.axis_index("x")
    m = zl * NC + co
    pos = yy * NM + m
    z12 = zl * NZH + zh

    def height_id(p):
        return {"y": p // NM, "zl": (p // NC) % NZL, "core": p % NC}

    has_prev, has_next = pos > 0, pos < NH - 1
    prev_id, next_id = height_id(jnp.maximum(pos - 1, 0)), height_id(jnp.minimum(pos + 1, NH - 1))

    cp_xc = pltpu.make_async_copy(xc_in.at[0], xcr.at[pl.ds(1, 2)], lsem.at[0])
    cp_k = pltpu.make_async_copy(k_in, kv, lsem.at[1])
    cp_xn = pltpu.make_async_copy(xn_in.at[0], xnr.at[pl.ds(1, 2)], lsem.at[2])
    cp_go = pltpu.make_async_copy(go_in.at[0], gor, lsem.at[3])
    for cp in (cp_xc, cp_k, cp_xn, cp_go):
        cp.start()

    barrier = pltpu.get_barrier_semaphore()

    def greet(device_id):
        pl.semaphore_signal(barrier, inc=1, device_id=device_id, device_id_type=pl.DeviceIdType.MESH)

    @pl.when(has_prev)
    def _():
        greet(prev_id)

    @pl.when(has_next)
    def _():
        greet(next_id)

    def far_z(i, c):
        greet({"zl": i, "zh": 1 - zh})
        return c

    lax.fori_loop(0, NZL, far_z, 0)

    def far_m(i, c):
        t = (m + i) % NM
        greet({"zl": t // NC, "core": t % NC})
        return c

    lax.fori_loop(1, NM, far_m, 0)

    def far_y(i, c):
        greet({"y": (yy + i) % NY})
        return c

    lax.fori_loop(1, NY, far_y, 0)

    def far_x(i, c):
        greet({"x": (xx + i) % NX})
        return c

    lax.fori_loop(1, NX, far_x, 0)

    rows_i = lax.broadcasted_iota(jnp.int32, (CH, COLS), 0)
    lane_i = lax.broadcasted_iota(jnp.int32, (CH, COLS), 1)
    rel = rows_i - GROUP * (lane_i & 31)
    emask[...] = jnp.where((rel >= 0) & (rel < GROUP), 1.0, 0.0).astype(f32)
    eye = lax.broadcasted_iota(jnp.int32, (CH, CH), 0) == lax.broadcasted_iota(jnp.int32, (CH, CH), 1)
    gam[...] = jnp.sum(jnp.where(eye, gam_in[...], 0.0), axis=1, keepdims=True)
    bet[...] = jnp.sum(jnp.where(eye, bet_in[...], 0.0), axis=1, keepdims=True)
    zc[...] = jnp.zeros_like(zc)
    zn[...] = jnp.zeros_like(zn)
    for b in range(3):
        for r in range(4):
            xcs[b, r, CH:, :] = jnp.zeros((PAD - CH, COLS), bf16)

    lane = lax.broadcasted_iota(jnp.int32, (CH, COLS), 1)

    def put_shifts(dst, row, v):
        wide = v.astype(f32)
        dst[0, row, :CH, :] = jnp.where(lane == 0, 0.0, pltpu.roll(wide, 1, 1)).astype(bf16)
        dst[1, row, :CH, :] = v
        dst[2, row, :CH, :] = jnp.where(lane == COLS - 1, 0.0, pltpu.roll(wide, COLS - 1, 1)).astype(bf16)

    cp_xc.wait()
    put_shifts(xcs, 1, xcr[1])
    put_shifts(xcs, 2, xcr[2])

    core27 = NZL + (NM - 1) + (NY - 1) + (NX - 1)
    pl.semaphore_wait(barrier, core27 + has_prev.astype(jnp.int32) + has_next.astype(jnp.int32))

    def halo(src, dst, to_next, i, send, recv):
        return pltpu.make_async_remote_copy(
            src_ref=src.at[0, 1] if to_next else src.at[0, 0],
            dst_ref=dst.at[0] if to_next else dst.at[3],
            send_sem=send.at[i],
            recv_sem=recv.at[i],
            device_id=next_id if to_next else prev_id,
            device_id_type=pl.DeviceIdType.MESH,
        )

    halos = (
        halo(xc_in, xcr, True, 0, hs, hr),
        halo(xc_in, xcr, False, 1, hs, hr),
        halo(xn_in, xnr, True, 2, hs, hr),
        halo(xn_in, xnr, False, 3, hs, hr),
    )

    @pl.when(has_next)
    def _():
        halos[0].start()

    @pl.when(has_prev)
    def _():
        halos[1].start()

    @pl.when(has_next)
    def _():
        halos[2].start()

    @pl.when(has_prev)
    def _():
        halos[3].start()

    cp_k.wait()

    def inner(b, c):
        x1, x2 = xcs[b, 1, :CH], xcs[b, 2, :CH]
        zc[...] += dot(kv[1, b], jnp.concatenate([x1, x2], axis=1))
        zc[:, COLS:] += dot(kv[0, b], x1)
        zc[:, :COLS] += dot(kv[2, b], x2)
        return c

    lax.fori_loop(0, 3, inner, 0)

    for b in range(3):
        n = BLOCKS[b] * 32
        rho = lax.broadcasted_iota(jnp.int32, (n, CH), 0)
        col = lax.broadcasted_iota(jnp.int32, (n, CH), 1)
        part = ((rho >> 3) & 3) * 4 + (rho & 3)
        src = 30 * (FIRST[b] + (rho >> 5)) + 15 * ((rho >> 2) & 1) + part - CH * b
        selm[b, :n, :] = jnp.where((part < 15) & (src == col), 1.0, 0.0).astype(bf16)

    def halo_wait(raw, shifted, up, down):
        @pl.when(has_prev)
        def _():
            up.wait_recv()

        @pl.when(jnp.logical_not(has_prev))
        def _():
            raw[0] = jnp.zeros((CH, COLS), bf16)

        @pl.when(has_next)
        def _():
            down.wait_recv()

        @pl.when(jnp.logical_not(has_next))
        def _():
            raw[3] = jnp.zeros((CH, COLS), bf16)

        put_shifts(shifted, 0, raw[0])
        put_shifts(shifted, 3, raw[3])

    halo_wait(xcr, xcs, halos[0], halos[1])

    def outer(b, c):
        zc[:, :COLS] += dot(kv[0, b], xcs[b, 0, :CH])
        zc[:, COLS:] += dot(kv[2, b], xcs[b, 3, :CH])
        return c

    lax.fori_loop(0, 3, outer, 0)

    def tile_of(cols4):
        q = lane >> 5
        picked = jnp.zeros((CH, COLS), f32)
        for i, v in enumerate(cols4):
            picked = jnp.where(q == i, v, picked)
        return jnp.sum((picked * emask[...]).reshape(CH // 8, 8, COLS), axis=0)

    def a_copy(buf, send, recv, i, slot, t):
        return pltpu.make_async_remote_copy(
            src_ref=buf.at[slot],
            dst_ref=buf.at[slot],
            send_sem=send.at[i],
            recv_sem=recv.at[slot],
            device_id={"zl": t // NC, "core": t % NC},
            device_id_type=pl.DeviceIdType.MESH,
        )

    def b_copy(buf, send, recv, i, slot, t):
        return pltpu.make_async_remote_copy(
            src_ref=buf.at[slot],
            dst_ref=buf.at[slot],
            send_sem=send.at[i],
            recv_sem=recv.at[slot],
            device_id={"y": t},
            device_id_type=pl.DeviceIdType.MESH,
        )

    def start_all(copy, buf, send, recv, me, n, tile):
        buf[me] = tile

        def go(i, c):
            copy(buf, send, recv, i, me, (me + i) % n).start()
            return c

        lax.fori_loop(1, n, go, 0)

    def wait_all(copy, buf, send, recv, me, n):
        def go(i, c):
            t = (me + i) % n
            copy(buf, send, recv, i, t, t).wait_recv()
            return c

        lax.fori_loop(1, n, go, 0)
        return jnp.sum(buf[...], axis=0)

    def sent_all(copy, buf, send, recv, me, n):
        def go(i, c):
            copy(buf, send, recv, i, me, (me + i) % n).wait_send()
            return c

        lax.fori_loop(1, n, go, 0)

    z = zc[...]
    start_all(
        a_copy, ra, as_, ar, m, NM,
        tile_of((jnp.sum(z, axis=1, keepdims=True), jnp.sum(z * z, axis=1, keepdims=True))),
    )

    cp_xn.wait()
    put_shifts(xns, 1, xnr[1])
    put_shifts(xns, 2, xnr[2])
    halo_wait(xnr, xns, halos[2], halos[3])

    def whole(t, c):
        a, b = t // 3, t % 3
        zn[...] += dot(
            kv[a, b], jnp.concatenate([xns[b, a, :CH], xns[b, a + 1, :CH]], axis=1)
        )
        return c

    lax.fori_loop(0, 5, whole, 0)
    start_all(b_copy, rb, bs, br, yy, NY, wait_all(a_copy, ra, as_, ar, m, NM))
    lax.fori_loop(5, 9, whole, 0)
    zv = zn[...]
    next_sums = (jnp.sum(zv, axis=1, keepdims=True), jnp.sum(zv * zv, axis=1, keepdims=True))
    cp_go.wait()
    total = wait_all(b_copy, rb, bs, br, yy, NY)

    def column(row, block):
        keep = (lane >> 5) == block
        return jnp.sum(jnp.where(keep, emask[...] * row, 0.0), axis=1, keepdims=True)

    def moments(tile, first):
        row = jnp.sum(tile, axis=0, keepdims=True) / COUNT
        mean_row = pltpu.roll(jnp.broadcast_to(row, (8, COLS)), (128 - 32 * first) % 128, 1)[:1]
        square_row = pltpu.roll(jnp.broadcast_to(row, (8, COLS)), (128 - 32 * (first + 1)) % 128, 1)[:1]
        rstd_row = lax.rsqrt(square_row - mean_row * mean_row + EPS)
        return column(mean_row, 0), column(rstd_row, 0)

    mean_c, rstd_c = moments(total, 0)
    normed = (zc[...] - mean_c) * rstd_c
    nrm[...] = normed
    affine = normed * gam[...] + bet[...]
    sig = jax.nn.sigmoid(affine)
    grad = jnp.concatenate([gor[0], gor[1]], axis=1).astype(f32)
    grad_n = grad * (sig * (1.0 + affine * (1.0 - sig))) * gam[...]
    gn[...] = grad_n
    start_all(
        a_copy, ra2, as2, ar2, m, NM,
        tile_of(
            (
                jnp.sum(grad_n, axis=1, keepdims=True),
                jnp.sum(grad_n * normed, axis=1, keepdims=True),
            )
            + next_sums
        ),
    )
    start_all(b_copy, rb2, bs2, br2, yy, NY, wait_all(a_copy, ra2, as2, ar2, m, NM))
    total2 = wait_all(b_copy, rb2, bs2, br2, yy, NY)
    row2 = jnp.sum(total2, axis=0, keepdims=True) / COUNT
    mean_1, mean_2 = column(row2, 0), column(row2, 1)
    gz = (rstd_c * (gn[...] - mean_1 - nrm[...] * mean_2)).astype(bf16)
    gzo[0] = gz[:, :COLS]
    gzo[1] = gz[:, COLS:]

    def gz_copy(to_next):
        return pltpu.make_async_remote_copy(
            src_ref=gzo.at[1] if to_next else gzo.at[0],
            dst_ref=gzh.at[0] if to_next else gzh.at[1],
            send_sem=ghs.at[0 if to_next else 1],
            recv_sem=ghr.at[0 if to_next else 1],
            device_id=next_id if to_next else prev_id,
            device_id_type=pl.DeviceIdType.MESH,
        )

    gz_next, gz_prev = gz_copy(True), gz_copy(False)

    @pl.when(has_next)
    def _():
        gz_next.start()

    @pl.when(has_prev)
    def _():
        gz_prev.start()

    picked = [dot(selm[b, : BLOCKS[b] * 32], gz).astype(bf16) for b in range(3)]
    for a in range(3):
        for b in range(3):
            source = jnp.concatenate([xcs[b, a], xcs[b, a + 1]], axis=1)
            out = dot(picked[b], source, NT)
            for d in range(BLOCKS[b]):
                block = 32 * a + FIRST[b] + d
                where = (block // 2) % NZL, block % 2
                rows = slice(block // NM * 8, block // NM * 8 + 8)
                for u in range(NX):
                    piece = out[d * 32 + u * 8 : d * 32 + u * 8 + 8]
                    if d == 0 and b > 0:
                        gacc[where[0], where[1], u, rows, :] += piece
                    else:
                        gacc[where[0], where[1], u, rows, :] = piece

    def send_core(k):
        return pltpu.make_async_remote_copy(
            src_ref=s1.at[k], dst_ref=r1.at[k], send_sem=c1s.at[k], recv_sem=c1r.at[k],
            device_id={"core": 1 - co}, device_id_type=pl.DeviceIdType.MESH,
        )

    pair = xx + 1 - 2 * (xx % 2)
    mirror = 3 - xx

    def partners(k):
        return (pair, mirror) if k < 3 else (mirror, pair)

    def second_of_first(k):
        first = partners(k)[0]
        return 3 - first if k < 3 else first + 1 - 2 * (first % 2)

    def send_x1(k):
        return pltpu.make_async_remote_copy(
            src_ref=s2.at[k], dst_ref=r2.at[k], send_sem=c2s.at[k], recv_sem=c2r.at[k],
            device_id={"x": partners(k)[0]}, device_id_type=pl.DeviceIdType.MESH,
        )

    def send_x2(k):
        return pltpu.make_async_remote_copy(
            src_ref=s3.at[k], dst_ref=r3.at[k], send_sem=c3s.at[k], recv_sem=c3r.at[k],
            device_id={"x": partners(k)[1]}, device_id_type=pl.DeviceIdType.MESH,
        )

    def y_copy(k, i, slot, src, t):
        return pltpu.make_async_remote_copy(
            src_ref=s4.at[k, src], dst_ref=r4.at[k, slot], send_sem=c4s.at[k, i],
            recv_sem=c4r.at[k, slot], device_id={"y": t}, device_id_type=pl.DeviceIdType.MESH,
        )

    def z_copy(k, h, slot):
        return pltpu.make_async_remote_copy(
            src_ref=s5.at[k], dst_ref=r5.at[slot], send_sem=c5s.at[k, h], recv_sem=c5r.at[slot],
            device_id={"zl": k, "zh": h}, device_id_type=pl.DeviceIdType.MESH,
        )

    def g_copy(i, slot, t):
        return pltpu.make_async_remote_copy(
            src_ref=r6.at[slot], dst_ref=r6.at[slot], send_sem=c6s.at[i], recv_sem=c6r.at[slot],
            device_id={"x": t}, device_id_type=pl.DeviceIdType.MESH,
        )

    def summed(k, u):
        return gacc[k, co, u] + r1[k, u].astype(f32)

    def step_x1(k):
        send_core(k).wait_recv()
        s2[k, 0] = summed(k, partners(k)[0]).astype(bf16)
        s2[k, 1] = summed(k, second_of_first(k)).astype(bf16)
        send_x1(k).start()

    def step_x2(k):
        send_x1(k).wait_recv()
        s3[k] = (summed(k, partners(k)[1]) + r2[k, 1].astype(f32)).astype(bf16)
        send_x2(k).start()

    def step_y(k):
        send_x2(k).wait_recv()
        val = (summed(k, xx) + r2[k, 0].astype(f32) + r3[k].astype(f32)).reshape(NY, 8, PAD)
        bown[k] = val
        s4[k] = val.astype(bf16)

        def go(i, c):
            t = (yy + i) % NY
            y_copy(k, i, yy, t, t).start()
            return c

        lax.fori_loop(1, NY, go, 0)

    def step_z(k):
        def go(i, acc):
            t = (yy + i) % NY
            y_copy(k, i, t, t, t).wait_recv()
            return acc + r4[k, t].astype(f32)

        val = lax.fori_loop(1, NY, go, bown[k, yy])
        cown[k] = val
        s5[k] = val.astype(bf16)
        for h in range(NZH):
            @pl.when(jnp.logical_or(zl != k, zh != h))
            def _():
                z_copy(k, h, z12).start()

    for k in ORDER:
        s1[k] = gacc[k, 1 - co].astype(bf16)
        send_core(k).start()

    row_n = jnp.sum(total2, axis=0, keepdims=True) / COUNT
    mean_n = column(row_n, 2)
    square_n = column(row_n, 3)
    rstd_n = lax.rsqrt(square_n - mean_n * mean_n + EPS)
    affine_n = (zn[...] - mean_n) * rstd_n * gam[...] + bet[...]
    y_next = (affine_n * jax.nn.sigmoid(affine_n)).astype(bf16)
    y_out[0, 0] = y_next[:, :COLS]
    y_out[0, 1] = y_next[:, COLS:]

    for k in ORDER:
        step_x1(k)

    @pl.when(has_prev)
    def _():
        gz_next.wait_recv()

    @pl.when(jnp.logical_not(has_prev))
    def _():
        gzh[0] = jnp.zeros((CH, COLS), bf16)

    @pl.when(has_next)
    def _():
        gz_prev.wait_recv()

    @pl.when(jnp.logical_not(has_next))
    def _():
        gzh[1] = jnp.zeros((CH, COLS), bf16)

    put_shifts(gzs, 0, gzh[0])
    put_shifts(gzs, 1, gzo[0])
    put_shifts(gzs, 2, gzo[1])
    put_shifts(gzs, 3, gzh[1])
    zc[...] = jnp.zeros_like(zc)

    def back(t, c):
        a, b = t // 3, t % 3
        source = jnp.concatenate([gzs[2 - b, 2 - a, :CH], gzs[2 - b, 3 - a, :CH]], axis=1)
        zc[...] += dot(kv[a, b], source, TN)
        return c

    lax.fori_loop(0, 9, back, 0)
    grad_x = zc[...].astype(bf16)
    gx_out[0, 0] = grad_x[:, :COLS]
    gx_out[0, 1] = grad_x[:, COLS:]

    for step in range(len(ORDER) + 5):
        if step < 6:
            step_x2(ORDER[step])
        if 2 <= step < 8:
            step_y(ORDER[step - 2])
        if 5 <= step < 11:
            step_z(ORDER[step - 5])

    def gather_z(i, acc):
        t = (z12 + i) % NZ
        z_copy(0, 0, t).wait_recv()
        return acc + r5[t].astype(f32)

    final = lax.fori_loop(1, NZ, gather_z, cown[zl])
    r6[xx] = final

    def go_x(i, c):
        g_copy(i, xx, (xx + i) % NX).start()
        return c

    lax.fori_loop(1, NX, go_x, 0)

    @pl.when(has_next)
    def _():
        halos[0].wait_send()
        halos[2].wait_send()
        gz_next.wait_send()

    @pl.when(has_prev)
    def _():
        halos[1].wait_send()
        halos[3].wait_send()
        gz_prev.wait_send()

    sent_all(a_copy, ra, as_, ar, m, NM)
    sent_all(b_copy, rb, bs, br, yy, NY)
    sent_all(a_copy, ra2, as2, ar2, m, NM)
    sent_all(b_copy, rb2, bs2, br2, yy, NY)
    for k in range(NZL):
        send_core(k).wait_send()
        send_x1(k).wait_send()
        send_x2(k).wait_send()

        def sent_y(i, c):
            y_copy(k, i, yy, (yy + i) % NY, (yy + i) % NY).wait_send()
            return c

        lax.fori_loop(1, NY, sent_y, 0)
        for h in range(NZH):
            @pl.when(jnp.logical_or(zl != k, zh != h))
            def _():
                z_copy(k, h, z12).wait_send()

    def end_x(i, c):
        t = (xx + i) % NX
        g_copy(i, t, t).wait_recv()
        g_copy(i, xx, t).wait_send()
        return c

    lax.fori_loop(1, NX, end_x, 0)
    gk_out[...] = r6[...]


def local(x_next, x_cur, grad_out, kernel, gamma, beta):
    any_spec = pl.BlockSpec(memory_space=pl.ANY)
    vmem = pl.BlockSpec(memory_space=pltpu.VMEM)
    dma = pltpu.SemaphoreType.DMA
    V = pltpu.VMEM
    scratch = [
        V((4, CH, COLS), bf16), V((4, CH, COLS), bf16), V((2, CH, COLS), bf16),
        V((3, 3, CH, CH), bf16),
        V((3, 4, PAD, COLS), bf16), V((3, 4, CH, COLS), bf16),
        V((2, CH, COLS), bf16), V((2, CH, COLS), bf16), V((3, 4, CH, COLS), bf16),
        V((CH, 2 * COLS), f32), V((CH, 2 * COLS), f32), V((CH, 2 * COLS), f32), V((CH, 2 * COLS), f32),
        V((CH, COLS), f32), V((CH, 1), f32), V((CH, 1), f32),
        V((3, 32 * max(BLOCKS), CH), bf16),
        V((NM, 8, COLS), f32), V((NY, 8, COLS), f32), V((NM, 8, COLS), f32), V((NY, 8, COLS), f32),
        V((NZL, NC, NX, NY * 8, PAD), f32),
        V((NZL, NX, NY * 8, PAD), bf16), V((NZL, NX, NY * 8, PAD), bf16),
        V((NZL, 2, NY * 8, PAD), bf16), V((NZL, 2, NY * 8, PAD), bf16),
        V((NZL, NY * 8, PAD), bf16), V((NZL, NY * 8, PAD), bf16),
        V((NZL, NY, 8, PAD), bf16), V((NZL, NY, 8, PAD), bf16),
        V((NZL, NY, 8, PAD), f32),
        V((NZL, 8, PAD), bf16), V((NZL, 8, PAD), f32),
        V((NZ, 8, PAD), bf16), V((NX, 8, PAD), f32),
        dma((4,)), dma((4,)), dma((4,)), dma((2,)), dma((2,)),
        dma((NM,)), dma((NM,)), dma((NY,)), dma((NY,)),
        dma((NM,)), dma((NM,)), dma((NY,)), dma((NY,)),
        dma((NZL,)), dma((NZL,)), dma((NZL,)), dma((NZL,)), dma((NZL,)), dma((NZL,)),
        dma((NZL, NY)), dma((NZL, NY)), dma((NZL, NZH)), dma((NZ,)), dma((NX,)), dma((NX,)),
    ]
    y_next, grad_x, quarters = pl.pallas_call(
        body,
        out_shape=(
            jax.ShapeDtypeStruct(x_next.shape, bf16),
            jax.ShapeDtypeStruct(x_next.shape, bf16),
            jax.ShapeDtypeStruct((NX, 8, PAD), f32),
        ),
        in_specs=[any_spec, any_spec, any_spec, any_spec, vmem, vmem],
        out_specs=(vmem, vmem, vmem),
        scratch_shapes=scratch,
        compiler_params=pltpu.CompilerParams(
            collective_id=0, has_side_effects=True, vmem_limit_bytes=60 * 1024 * 1024
        ),
    )(x_next, x_cur, grad_out, kernel, gamma.reshape(1, CH), beta.reshape(1, CH))
    half = lax.dynamic_slice_in_dim(
        quarters.reshape(NX, NZH, 4, PAD), lax.axis_index("zh"), 1, axis=1
    )
    flat = half[:, 0, :, :CH].reshape(-1)
    grad_kernel = lax.dynamic_slice_in_dim(flat, 1200 * lax.axis_index("x"), 1200)
    return y_next, grad_x, grad_kernel


def solution(mesh):
    torus = Mesh(mesh.devices.reshape(NY, NZL, NC, NZH, NX), HEIGHT + DP)
    image = P(DP, HEIGHT, None, None)
    return jax.shard_map(
        local,
        mesh=torus,
        in_specs=(image, image, image, P(), P(), P()),
        out_specs=(image, image, P(HEIGHT + DP)),
        check_vma=False,
    )
```

time: 656 us -> 86.2 us (0.13)
  the two profiles are of different devices: /device:TPU:24 before, /device:TPU:128 now
where the time goes in v1:
time: 86.2 us; the launch traced here: 85.9 us
  Pallas kernels  78 us (90%)
  local copies, waits for them, and re-layouts  7.26 us (8%)
    pallas_call x1, Pallas kernels, local(): pl.pallas_call(body, out_shape=(jax.ShapeDtypeStruct(x_next.shape, bf16),...  78 us
    unnamed x2, local copies, waits for them, and re-layouts  3.18 us

profile of v1, /device:TPU:128, one launch (start us, length us, event | category | flops | bytes accessed | tf_op | source)
XLA Modules:
  0.0 85.9 jit_solution(2185728412131086105)
XLA Ops:
  0.6 1.2 %reshape.15.gam_in = f32[1,320]{1,0:T(1,128)} reshape(f32[320]{0:T(512)} %param.10) | data formatting | bytes 2560 | tf_op jit(solution)/shard_map/reshape | solution.py:604
  1.9 1.2 %reshape.16.bet_in = f32[1,320]{1,0:T(1,128)} reshape(f32[320]{0:T(512)} %param.11) | data formatting | bytes 2560 | tf_op jit(solution)/shard_map/reshape | solution.py:604
  3.1 78.0 %shard_map.85 = (bf16[1,2,320,128]{3,2,1,0:T(8,128)(2,1)}, bf16[1,2,320,128]{3,2,1,0:T(8,128)(2,1)}, f32[4,8,384]{2,1,0:T(8,128)}) custom-call(bf16[1,2,320,128]{3,2,1,0:T(8,128)(2,1)} %xn_in.1, bf16[1,2,320,128]{3,2,1,0:T(8,128)(2,1)} %xc_in.1, bf16[1,2,320,128]{3,2,1,0:T(8,128)(2,1)} %go_in.1, bf16[3,3,320,320]{3,2,1,0:T(8,128)(2,1)} %k_in.1, ...), custom_call_target="tpu_custom_call" | custom-call | tf_op jit(solution)/shard_map/pallas_call | solution.py:591
  81.1 0.8 reshape.17
  82.0 0.1 reshape_squeeze.3
  82.0 0.7 dynamic_slice.7
  82.7 1.6 %copy.11 = bf16[1,2,320,128]{3,2,1,0:T(8,128)(2,1)} copy(bf16[1,2,320,128]{3,2,1,0:T(8,128)(2,1)} %get-tuple-element.12) | data formatting | bytes 327680
  84.3 1.6 %copy.12 = bf16[1,2,320,128]{3,2,1,0:T(8,128)(2,1)} copy(bf16[1,2,320,128]{3,2,1,0:T(8,128)(2,1)} %get-tuple-element.13) | data formatting | bytes 327680
  (1 shorter events, 0.0 us)

commit v2 on v1

--- a/solution.py
+++ b/solution.py
@@ -8,7 +8,10 @@
 
 CH = 320
 COLS = 128
-PAD = 384
+LANES = 128
+MAIN = 256
+REST = CH - MAIN
+TALL = 160
 GROUP = 10
 NY, NZL, NC, NZH, NX = 8, 6, 2, 2, 4
 NM = NZL * NC
@@ -37,7 +40,7 @@
 def body(
     xn_in, xc_in, go_in, k_in, gam_in, bet_in,
     y_out, gx_out, gk_out,
-    xcr, xnr, gor, kv, xcs, xns, gzo, gzh, gzs,
+    xcr, xnr, gor, kv, xcs, xhi, xns, gzo, gzh, gzs,
     zc, zn, nrm, gn, emask, gam, bet, selm,
     ra, rb, ra2, rb2,
     gacc, s1, r1, s2, r2, s3, r3, s4, r4, bown, s5, cown, r5, r6,
@@ -56,6 +59,44 @@
     has_prev, has_next = pos > 0, pos < NH - 1
     prev_id, next_id = height_id(jnp.maximum(pos - 1, 0)), height_id(jnp.minimum(pos + 1, NH - 1))
 
+    barrier = pltpu.get_barrier_semaphore()
+
+    def greet(device_id):
+        pl.semaphore_signal(barrier, inc=1, device_id=device_id, device_id_type=pl.DeviceIdType.MESH)
+
+    @pl.when(has_prev)
+    def _():
+        greet(prev_id)
+
+    @pl.when(has_next)
+    def _():
+        greet(next_id)
+
+    def far_z(i, c):
+        greet({"zl": i, "zh": 1 - zh})
+        return c
+
+    lax.fori_loop(0, NZL, far_z, 0)
+
+    def far_m(i, c):
+        t = (m + i) % NM
+        greet({"zl": t // NC, "core": t % NC})
+        return c
+
+    lax.fori_loop(1, NM, far_m, 0)
+
+    def far_y(i, c):
+        greet({"y": (yy + i) % NY})
+        return c
+
+    lax.fori_loop(1, NY, far_y, 0)
+
+    def far_x(i, c):
+        greet({"x": (xx + i) % NX})
+        return c
+
+    lax.fori_loop(1, NX, far_x, 0)
+
     cp_xc = pltpu.make_async_copy(xc_in.at[0], xcr.at[pl.ds(1, 2)], lsem.at[0])
     cp_k = pltpu.make_async_copy(k_in, kv, lsem.at[1])
     cp_xn = pltpu.make_async_copy(xn_in.at[0], xnr.at[pl.ds(1, 2)], lsem.at[2])
@@ -63,68 +104,37 @@
     for cp in (cp_xc, cp_k, cp_xn, cp_go):
         cp.start()
 
-    barrier = pltpu.get_barrier_semaphore()
-
-    def greet(device_id):
-        pl.semaphore_signal(barrier, inc=1, device_id=device_id, device_id_type=pl.DeviceIdType.MESH)
-
-    @pl.when(has_prev)
-    def _():
-        greet(prev_id)
-
-    @pl.when(has_next)
-    def _():
-        greet(next_id)
-
-    def far_z(i, c):
-        greet({"zl": i, "zh": 1 - zh})
-        return c
-
-    lax.fori_loop(0, NZL, far_z, 0)
-
-    def far_m(i, c):
-        t = (m + i) % NM
-        greet({"zl": t // NC, "core": t % NC})
-        return c
-
-    lax.fori_loop(1, NM, far_m, 0)
-
-    def far_y(i, c):
-        greet({"y": (yy + i) % NY})
-        return c
-
-    lax.fori_loop(1, NY, far_y, 0)
-
-    def far_x(i, c):
-        greet({"x": (xx + i) % NX})
-        return c
-
-    lax.fori_loop(1, NX, far_x, 0)
-
     rows_i = lax.broadcasted_iota(jnp.int32, (CH, COLS), 0)
     lane_i = lax.broadcasted_iota(jnp.int32, (CH, COLS), 1)
     rel = rows_i - GROUP * (lane_i & 31)
     emask[...] = jnp.where((rel >= 0) & (rel < GROUP), 1.0, 0.0).astype(f32)
     eye = lax.broadcasted_iota(jnp.int32, (CH, CH), 0) == lax.broadcasted_iota(jnp.int32, (CH, CH), 1)
-    gam[...] = jnp.sum(jnp.where(eye, gam_in[...], 0.0), axis=1, keepdims=True)
-    bet[...] = jnp.sum(jnp.where(eye, bet_in[...], 0.0), axis=1, keepdims=True)
+    gam[...] = jnp.sum(jnp.where(eye, gam_in[...].reshape(1, CH), 0.0), axis=1, keepdims=True)
+    bet[...] = jnp.sum(jnp.where(eye, bet_in[...].reshape(1, CH), 0.0), axis=1, keepdims=True)
     zc[...] = jnp.zeros_like(zc)
     zn[...] = jnp.zeros_like(zn)
     for b in range(3):
         for r in range(4):
-            xcs[b, r, CH:, :] = jnp.zeros((PAD - CH, COLS), bf16)
+            xcs[b, r, CH:, :] = jnp.zeros((REST, COLS), bf16)
+            xhi[b, r, :REST, :] = jnp.zeros((REST, COLS), bf16)
 
     lane = lax.broadcasted_iota(jnp.int32, (CH, COLS), 1)
 
-    def put_shifts(dst, row, v):
+    def put_shifts(dst, row, v, high=None):
         wide = v.astype(f32)
-        dst[0, row, :CH, :] = jnp.where(lane == 0, 0.0, pltpu.roll(wide, 1, 1)).astype(bf16)
-        dst[1, row, :CH, :] = v
-        dst[2, row, :CH, :] = jnp.where(lane == COLS - 1, 0.0, pltpu.roll(wide, COLS - 1, 1)).astype(bf16)
+        moved = (
+            jnp.where(lane == 0, 0.0, pltpu.roll(wide, 1, 1)).astype(bf16),
+            v,
+            jnp.where(lane == COLS - 1, 0.0, pltpu.roll(wide, COLS - 1, 1)).astype(bf16),
+        )
+        for b in range(3):
+            dst[b, row, :CH, :] = moved[b]
+            if high is not None:
+                high[b, row, REST:, :] = moved[b][MAIN:]
 
     cp_xc.wait()
-    put_shifts(xcs, 1, xcr[1])
-    put_shifts(xcs, 2, xcr[2])
+    put_shifts(xcs, 1, xcr[1], xhi)
+    put_shifts(xcs, 2, xcr[2], xhi)
 
     core27 = NZL + (NM - 1) + (NY - 1) + (NX - 1)
     pl.semaphore_wait(barrier, core27 + has_prev.astype(jnp.int32) + has_next.astype(jnp.int32))
@@ -154,24 +164,27 @@
     def _():
         halos[1].start()
 
-    @pl.when(has_next)
-    def _():
-        halos[2].start()
-
-    @pl.when(has_prev)
-    def _():
-        halos[3].start()
-
     cp_k.wait()
 
-    def inner(b, c):
-        x1, x2 = xcs[b, 1, :CH], xcs[b, 2, :CH]
-        zc[...] += dot(kv[1, b], jnp.concatenate([x1, x2], axis=1))
-        zc[:, COLS:] += dot(kv[0, b], x1)
-        zc[:, :COLS] += dot(kv[2, b], x2)
-        return c
-
-    lax.fori_loop(0, 3, inner, 0)
+    def conv_inner(acc, xs):
+        def go(b, c):
+            x1, x2 = xs[b, 1, :CH], xs[b, 2, :CH]
+            acc[...] += dot(kv[1, b], jnp.concatenate([x1, x2], axis=1))
+            acc[:, COLS:] += dot(kv[0, b], x1)
+            acc[:, :COLS] += dot(kv[2, b], x2)
+            return c
+
+        lax.fori_loop(0, 3, go, 0)
+
+    def conv_outer(acc, xs):
+        def go(b, c):
+            acc[:, :COLS] += dot(kv[0, b], xs[b, 0, :CH])
+            acc[:, COLS:] += dot(kv[2, b], xs[b, 3, :CH])
+            return c
+
+        lax.fori_loop(0, 3, go, 0)
+
+    conv_inner(zc, xcs)
 
     for b in range(3):
         n = BLOCKS[b] * 32
@@ -181,7 +194,7 @@
         src = 30 * (FIRST[b] + (rho >> 5)) + 15 * ((rho >> 2) & 1) + part - CH * b
         selm[b, :n, :] = jnp.where((part < 15) & (src == col), 1.0, 0.0).astype(bf16)
 
-    def halo_wait(raw, shifted, up, down):
+    def halo_wait(raw, up, down):
         @pl.when(has_prev)
         def _():
             up.wait_recv()
@@ -198,24 +211,26 @@
         def _():
             raw[3] = jnp.zeros((CH, COLS), bf16)
 
-        put_shifts(shifted, 0, raw[0])
-        put_shifts(shifted, 3, raw[3])
-
-    halo_wait(xcr, xcs, halos[0], halos[1])
-
-    def outer(b, c):
-        zc[:, :COLS] += dot(kv[0, b], xcs[b, 0, :CH])
-        zc[:, COLS:] += dot(kv[2, b], xcs[b, 3, :CH])
-        return c
-
-    lax.fori_loop(0, 3, outer, 0)
+    halo_wait(xcr, halos[0], halos[1])
+
+    @pl.when(has_next)
+    def _():
+        halos[2].start()
+
+    @pl.when(has_prev)
+    def _():
+        halos[3].start()
+
+    put_shifts(xcs, 0, xcr[0], xhi)
+    put_shifts(xcs, 3, xcr[3], xhi)
+    conv_outer(zc, xcs)
 
     def tile_of(cols4):
         q = lane >> 5
         picked = jnp.zeros((CH, COLS), f32)
         for i, v in enumerate(cols4):
             picked = jnp.where(q == i, v, picked)
-        return jnp.sum((picked * emask[...]).reshape(CH // 8, 8, COLS), axis=0)
+        return jnp.sum(picked * emask[...], axis=0, keepdims=True)
 
     def a_copy(buf, send, recv, i, slot, t):
         return pltpu.make_async_remote_copy(
@@ -271,18 +286,12 @@
     cp_xn.wait()
     put_shifts(xns, 1, xnr[1])
     put_shifts(xns, 2, xnr[2])
-    halo_wait(xnr, xns, halos[2], halos[3])
-
-    def whole(t, c):
-        a, b = t // 3, t % 3
-        zn[...] += dot(
-            kv[a, b], jnp.concatenate([xns[b, a, :CH], xns[b, a + 1, :CH]], axis=1)
-        )
-        return c
-
-    lax.fori_loop(0, 5, whole, 0)
+    conv_inner(zn, xns)
     start_all(b_copy, rb, bs, br, yy, NY, wait_all(a_copy, ra, as_, ar, m, NM))
-    lax.fori_loop(5, 9, whole, 0)
+    halo_wait(xnr, halos[2], halos[3])
+    put_shifts(xns, 0, xnr[0])
+    put_shifts(xns, 3, xnr[3])
+    conv_outer(zn, xns)
     zv = zn[...]
     next_sums = (jnp.sum(zv, axis=1, keepdims=True), jnp.sum(zv * zv, axis=1, keepdims=True))
     cp_go.wait()
@@ -293,7 +302,7 @@
         return jnp.sum(jnp.where(keep, emask[...] * row, 0.0), axis=1, keepdims=True)
 
     def moments(tile, first):
-        row = jnp.sum(tile, axis=0, keepdims=True) / COUNT
+        row = tile / COUNT
         mean_row = pltpu.roll(jnp.broadcast_to(row, (8, COLS)), (128 - 32 * first) % 128, 1)[:1]
         square_row = pltpu.roll(jnp.broadcast_to(row, (8, COLS)), (128 - 32 * (first + 1)) % 128, 1)[:1]
         rstd_row = lax.rsqrt(square_row - mean_row * mean_row + EPS)
@@ -319,7 +328,7 @@
     )
     start_all(b_copy, rb2, bs2, br2, yy, NY, wait_all(a_copy, ra2, as2, ar2, m, NM))
     total2 = wait_all(b_copy, rb2, bs2, br2, yy, NY)
-    row2 = jnp.sum(total2, axis=0, keepdims=True) / COUNT
+    row2 = total2 / COUNT
     mean_1, mean_2 = column(row2, 0), column(row2, 1)
     gz = (rstd_c * (gn[...] - mean_1 - nrm[...] * mean_2)).astype(bf16)
     gzo[0] = gz[:, :COLS]
@@ -346,20 +355,38 @@
         gz_prev.start()
 
     picked = [dot(selm[b, : BLOCKS[b] * 32], gz).astype(bf16) for b in range(3)]
+
+    def put(ref, rows, piece, add):
+        if add:
+            ref[rows, :] += piece
+        else:
+            ref[rows, :] = piece
+
     for a in range(3):
         for b in range(3):
-            source = jnp.concatenate([xcs[b, a], xcs[b, a + 1]], axis=1)
-            out = dot(picked[b], source, NT)
+            first = 32 * a + FIRST[b]
+            low = min(max(NH // 2 - first, 0), BLOCKS[b])
+            out = dot(picked[b], jnp.concatenate([xcs[b, a, :MAIN], xcs[b, a + 1, :MAIN]], axis=1), NT)
+            rest = []
+            if low > 0:
+                source = jnp.concatenate([xcs[b, a, MAIN:], xcs[b, a + 1, MAIN:]], axis=1)
+                rest.append(dot(picked[b][: low * 32], source, NT))
+            if low < BLOCKS[b]:
+                source = jnp.concatenate([xhi[b, a], xhi[b, a + 1]], axis=1)
+                rest.append(dot(picked[b][low * 32 :], source, NT))
             for d in range(BLOCKS[b]):
-                block = 32 * a + FIRST[b] + d
-                where = (block // 2) % NZL, block % 2
-                rows = slice(block // NM * 8, block // NM * 8 + 8)
+                block = first + d
+                row = block // NM
+                part, at = (rest[0], d) if d < low else (rest[-1], d - low)
+                again = d == 0 and b > 0
                 for u in range(NX):
-                    piece = out[d * 32 + u * 8 : d * 32 + u * 8 + 8]
-                    if d == 0 and b > 0:
-                        gacc[where[0], where[1], u, rows, :] += piece
-                    else:
-                        gacc[where[0], where[1], u, rows, :] = piece
+                    ref = gacc.at[(block // 2) % NZL, block % 2, u]
+                    top = d * 32 + u * 8
+                    put(ref, slice(row * 8, row * 8 + 8), out[top : top + 8, :LANES], again)
+                    put(ref, slice(64 + row * 8, 72 + row * 8), out[top : top + 8, LANES:], again)
+                    top = at * 32 + u * 8
+                    at_row = 128 + row % 4 * 8
+                    put(ref, slice(at_row, at_row + 8), part[top : top + 8], again or row >= 4)
 
     def send_core(k):
         return pltpu.make_async_remote_copy(
@@ -423,9 +450,13 @@
 
     def step_y(k):
         send_x2(k).wait_recv()
-        val = (summed(k, xx) + r2[k, 0].astype(f32) + r3[k].astype(f32)).reshape(NY, 8, PAD)
-        bown[k] = val
-        s4[k] = val.astype(bf16)
+        val = summed(k, xx) + r2[k, 0].astype(f32) + r3[k].astype(f32)
+        for i in range(2):
+            bown[k, :, i * 8 : i * 8 + 8, :] = val[i * 64 : i * 64 + 64].reshape(NY, 8, LANES)
+        rest = val[128:].reshape(NY // 2, 8, LANES)
+        bown[k, : NY // 2, 16:, :] = rest
+        bown[k, NY // 2 :, 16:, :] = rest
+        s4[k] = bown[k].astype(bf16)
 
         def go(i, c):
             t = (yy + i) % NY
@@ -452,9 +483,8 @@
         s1[k] = gacc[k, 1 - co].astype(bf16)
         send_core(k).start()
 
-    row_n = jnp.sum(total2, axis=0, keepdims=True) / COUNT
-    mean_n = column(row_n, 2)
-    square_n = column(row_n, 3)
+    mean_n = column(row2, 2)
+    square_n = column(row2, 3)
     rstd_n = lax.rsqrt(square_n - mean_n * mean_n + EPS)
     affine_n = (zn[...] - mean_n) * rstd_n * gam[...] + bet[...]
     y_next = (affine_n * jax.nn.sigmoid(affine_n)).astype(bf16)
@@ -560,6 +590,41 @@
     gk_out[...] = r6[...]
 
 
+def last(y_in, gx_in, raw, y_out, gx_out, gk_out, ybuf, gbuf, rows, sem):
+    pairs = ((y_in, ybuf, y_out), (gx_in, gbuf, gx_out))
+    into = [pltpu.make_async_copy(a, b, sem.at[i]) for i, (a, b, _) in enumerate(pairs)]
+    back = [pltpu.make_async_copy(b, c, sem.at[2 + i]) for i, (_, b, c) in enumerate(pairs)]
+    for cp in into:
+        cp.start()
+    second, high = lax.axis_index("zh") == 1, lax.axis_index("y") >= NY // 2
+    for u in range(NX):
+        tile = raw[u]
+        rest = tile[16:]
+        parts = (tile[:8], tile[8:16], jnp.where(high, pltpu.roll(rest, REST, 1), rest))
+        for i, p in enumerate(parts):
+            rows[u * 4 : u * 4 + 4, i * LANES : (i + 1) * LANES] = jnp.where(second, p[4:], p[:4])
+    into[0].wait()
+    back[0].start()
+    into[1].wait()
+    back[1].start()
+    share = 9 * CH * CH // (NH * NZH * NX)
+    for v in range(NX):
+
+        @pl.when(lax.axis_index("x") == v)
+        def _():
+            for start in range(0, share, LANES):
+                n = min(LANES, share - start)
+                r, col = divmod(share * v + start, CH)
+                k = min(n, CH - col)
+                piece = rows[r : r + 1, col : col + k]
+                if k < n:
+                    piece = jnp.concatenate([piece, rows[r + 1 : r + 2, : n - k]], axis=1)
+                gk_out[pl.ds(start, n)] = piece.reshape(n)
+
+    for cp in back:
+        cp.wait()
+
+
 def local(x_next, x_cur, grad_out, kernel, gamma, beta):
     any_spec = pl.BlockSpec(memory_space=pl.ANY)
     vmem = pl.BlockSpec(memory_space=pltpu.VMEM)
@@ -568,20 +633,20 @@
     scratch = [
         V((4, CH, COLS), bf16), V((4, CH, COLS), bf16), V((2, CH, COLS), bf16),
         V((3, 3, CH, CH), bf16),
-        V((3, 4, PAD, COLS), bf16), V((3, 4, CH, COLS), bf16),
+        V((3, 4, CH + REST, COLS), bf16), V((3, 4, 2 * REST, COLS), bf16), V((3, 4, CH, COLS), bf16),
         V((2, CH, COLS), bf16), V((2, CH, COLS), bf16), V((3, 4, CH, COLS), bf16),
         V((CH, 2 * COLS), f32), V((CH, 2 * COLS), f32), V((CH, 2 * COLS), f32), V((CH, 2 * COLS), f32),
         V((CH, COLS), f32), V((CH, 1), f32), V((CH, 1), f32),
         V((3, 32 * max(BLOCKS), CH), bf16),
-        V((NM, 8, COLS), f32), V((NY, 8, COLS), f32), V((NM, 8, COLS), f32), V((NY, 8, COLS), f32),
-        V((NZL, NC, NX, NY * 8, PAD), f32),
-        V((NZL, NX, NY * 8, PAD), bf16), V((NZL, NX, NY * 8, PAD), bf16),
-        V((NZL, 2, NY * 8, PAD), bf16), V((NZL, 2, NY * 8, PAD), bf16),
-        V((NZL, NY * 8, PAD), bf16), V((NZL, NY * 8, PAD), bf16),
-        V((NZL, NY, 8, PAD), bf16), V((NZL, NY, 8, PAD), bf16),
-        V((NZL, NY, 8, PAD), f32),
-        V((NZL, 8, PAD), bf16), V((NZL, 8, PAD), f32),
-        V((NZ, 8, PAD), bf16), V((NX, 8, PAD), f32),
+        V((NM, 1, COLS), f32), V((NY, 1, COLS), f32), V((NM, 1, COLS), f32), V((NY, 1, COLS), f32),
+        V((NZL, NC, NX, TALL, LANES), f32),
+        V((NZL, NX, TALL, LANES), bf16), V((NZL, NX, TALL, LANES), bf16),
+        V((NZL, 2, TALL, LANES), bf16), V((NZL, 2, TALL, LANES), bf16),
+        V((NZL, TALL, LANES), bf16), V((NZL, TALL, LANES), bf16),
+        V((NZL, NY, 24, LANES), bf16), V((NZL, NY, 24, LANES), bf16),
+        V((NZL, NY, 24, LANES), f32),
+        V((NZL, 24, LANES), bf16), V((NZL, 24, LANES), f32),
+        V((NZ, 24, LANES), bf16), V((NX, 24, LANES), f32),
         dma((4,)), dma((4,)), dma((4,)), dma((2,)), dma((2,)),
         dma((NM,)), dma((NM,)), dma((NY,)), dma((NY,)),
         dma((NM,)), dma((NM,)), dma((NY,)), dma((NY,)),
@@ -593,7 +658,7 @@
         out_shape=(
             jax.ShapeDtypeStruct(x_next.shape, bf16),
             jax.ShapeDtypeStruct(x_next.shape, bf16),
-            jax.ShapeDtypeStruct((NX, 8, PAD), f32),
+            jax.ShapeDtypeStruct((NX, 24, LANES), f32),
         ),
         in_specs=[any_spec, any_spec, any_spec, any_spec, vmem, vmem],
         out_specs=(vmem, vmem, vmem),
@@ -601,13 +666,18 @@
         compiler_params=pltpu.CompilerParams(
             collective_id=0, has_side_effects=True, vmem_limit_bytes=60 * 1024 * 1024
         ),
-    )(x_next, x_cur, grad_out, kernel, gamma.reshape(1, CH), beta.reshape(1, CH))
-    half = lax.dynamic_slice_in_dim(
-        quarters.reshape(NX, NZH, 4, PAD), lax.axis_index("zh"), 1, axis=1
-    )
-    flat = half[:, 0, :, :CH].reshape(-1)
-    grad_kernel = lax.dynamic_slice_in_dim(flat, 1200 * lax.axis_index("x"), 1200)
-    return y_next, grad_x, grad_kernel
+    )(x_next, x_cur, grad_out, kernel, gamma, beta)
+    return pl.pallas_call(
+        last,
+        out_shape=(
+            jax.ShapeDtypeStruct(x_next.shape, bf16),
+            jax.ShapeDtypeStruct(x_next.shape, bf16),
+            jax.ShapeDtypeStruct((9 * CH * CH // (NH * NZH * NX),), f32),
+        ),
+        in_specs=[any_spec, any_spec, vmem],
+        out_specs=(any_spec, any_spec, vmem),
+        scratch_shapes=[V(x_next.shape, bf16), V(x_next.shape, bf16), V((16, 3 * LANES), f32), dma((4,))],
+    )(y_next, grad_x, quarters)
 
 
 def solution(mesh):

time: 86.2 us -> 81 us (0.940)
  local copies, waits for them, and re-layouts: 7.26 us -> 0 us
  Pallas kernels: 78 us -> 80.2 us
    reshape x3 -> x0, local copies, waits for them, and re-layouts: 3.31 us -> none  [the longest x1 1.25 us: local(): gamma.reshape(1, CH)]
    unnamed x2 -> x0, local copies, waits for them, and re-layouts: 3.18 us -> none
    pallas_call x0 -> x1, Pallas kernels: none -> 3.09 us  [local(): pl.pallas_call(last, out_shape=(jax.ShapeDtypeStruct(x_next.shape, bf16),...]
    pallas_call x1, Pallas kernels: 78 us -> 77.1 us  [local(): pl.pallas_call(body, out_shape=(jax.ShapeDtypeStruct(x_next.shape, bf16),...]
where the time goes in v2:
time: 81 us; the launch traced here: 80.8 us
  Pallas kernels  80.2 us (99%)
    pallas_call x1, Pallas kernels, local(): pl.pallas_call(body, out_shape=(jax.ShapeDtypeStruct(x_next.shape, bf16),...  77.1 us
    pallas_call x1, Pallas kernels, local(): pl.pallas_call(last, out_shape=(jax.ShapeDtypeStruct(x_next.shape, bf16),...  3.09 us

profile of v2, /device:TPU:128, one launch (start us, length us, event | category | flops | bytes accessed | tf_op | source)
XLA Modules:
  0.0 80.8 jit_solution(10067838286472883594)
XLA Ops:
  0.6 77.1 %shard_map.85 = (bf16[1,2,320,128]{3,2,1,0:T(8,128)(2,1)}, bf16[1,2,320,128]{3,2,1,0:T(8,128)(2,1)}, f32[4,24,128]{2,1,0:T(8,128)}) custom-call(bf16[1,2,320,128]{3,2,1,0:T(8,128)(2,1)} %xn_in.1, bf16[1,2,320,128]{3,2,1,0:T(8,128)(2,1)} %xc_in.1, bf16[1,2,320,128]{3,2,1,0:T(8,128)(2,1)} %go_in.1, bf16[3,3,320,320]{3,2,1,0:T(8,128)(2,1)} %k_in.1, f32[320]{0:T(512)} %gam_in.1, ...), custom_call_target="tpu_custom_call" | custom-call | tf_op jit(solution)/shard_map/pallas_call | solution.py:656
  77.7 3.1 %shard_map.86 = (bf16[1,2,320,128]{3,2,1,0:T(8,128)(2,1)}, bf16[1,2,320,128]{3,2,1,0:T(8,128)(2,1)}, f32[1200]{0:T(1024)}) custom-call(bf16[1,2,320,128]{3,2,1,0:T(8,128)(2,1)} %get-tuple-element.6.y_in, bf16[1,2,320,128]{3,2,1,0:T(8,128)(2,1)} %get-tuple-element.7.gx_in, f32[4,24,128]{2,1,0:T(8,128)} %get-tuple-element.8.raw), custom_call_target="tpu_custom_call" | custom-call | tf_op jit(solution)/shard_map/pallas_call | solution.py:670

commit v3 on v2

--- a/solution.py
+++ b/solution.py
@@ -40,12 +40,12 @@
 def body(
     xn_in, xc_in, go_in, k_in, gam_in, bet_in,
     y_out, gx_out, gk_out,
-    xcr, xnr, gor, kv, xcs, xhi, xns, gzo, gzh, gzs,
+    gam_row, bet_row, xcr, xnr, gor, kv, xcs, xhi, xns, gzo, gzh, gzs,
     zc, zn, nrm, gn, emask, gam, bet, selm,
     ra, rb, ra2, rb2,
-    gacc, s1, r1, s2, r2, s3, r3, s4, r4, bown, s5, cown, r5, r6,
+    gacc, s1, r1, s2, r2, s3, r3, s4, r4, bown, s5, cown, r5, mine, before,
     lsem, hs, hr, ghs, ghr, as_, ar, bs, br, as2, ar2, bs2, br2,
-    c1s, c1r, c2s, c2r, c3s, c3r, c4s, c4r, c5s, c5r, c6s, c6r,
+    c1s, c1r, c2s, c2r, c3s, c3r, c4s, c4r, c5s, c5r, fsem,
 ):
     yy, zl, co = lax.axis_index("y"), lax.axis_index("zl"), lax.axis_index("core")
     zh, xx = lax.axis_index("zh"), lax.axis_index("x")
@@ -101,16 +101,48 @@
     cp_k = pltpu.make_async_copy(k_in, kv, lsem.at[1])
     cp_xn = pltpu.make_async_copy(xn_in.at[0], xnr.at[pl.ds(1, 2)], lsem.at[2])
     cp_go = pltpu.make_async_copy(go_in.at[0], gor, lsem.at[3])
-    for cp in (cp_xc, cp_k, cp_xn, cp_go):
+    cp_gam = pltpu.make_async_copy(gam_in, gam_row, lsem.at[4])
+    cp_bet = pltpu.make_async_copy(bet_in, bet_row, lsem.at[5])
+    for cp in (cp_xc, cp_gam, cp_bet, cp_k, cp_xn, cp_go):
         cp.start()
+
+    greeted = NZL + (NM - 1) + (NY - 1) + (NX - 1)
+    pl.semaphore_wait(barrier, greeted + has_prev.astype(jnp.int32) + has_next.astype(jnp.int32))
+
+    def halo(src, dst, to_next, i, send, recv):
+        return pltpu.make_async_remote_copy(
+            src_ref=src.at[0, 1] if to_next else src.at[0, 0],
+            dst_ref=dst.at[0] if to_next else dst.at[3],
+            send_sem=send.at[i],
+            recv_sem=recv.at[i],
+            device_id=next_id if to_next else prev_id,
+            device_id_type=pl.DeviceIdType.MESH,
+        )
+
+    halos = (
+        halo(xc_in, xcr, True, 0, hs, hr),
+        halo(xc_in, xcr, False, 1, hs, hr),
+        halo(xn_in, xnr, True, 2, hs, hr),
+        halo(xn_in, xnr, False, 3, hs, hr),
+    )
+
+    @pl.when(has_next)
+    def _():
+        halos[0].start()
+
+    @pl.when(has_prev)
+    def _():
+        halos[1].start()
 
     rows_i = lax.broadcasted_iota(jnp.int32, (CH, COLS), 0)
     lane_i = lax.broadcasted_iota(jnp.int32, (CH, COLS), 1)
     rel = rows_i - GROUP * (lane_i & 31)
     emask[...] = jnp.where((rel >= 0) & (rel < GROUP), 1.0, 0.0).astype(f32)
     eye = lax.broadcasted_iota(jnp.int32, (CH, CH), 0) == lax.broadcasted_iota(jnp.int32, (CH, CH), 1)
-    gam[...] = jnp.sum(jnp.where(eye, gam_in[...].reshape(1, CH), 0.0), axis=1, keepdims=True)
-    bet[...] = jnp.sum(jnp.where(eye, bet_in[...].reshape(1, CH), 0.0), axis=1, keepdims=True)
+    cp_gam.wait()
+    cp_bet.wait()
+    gam[...] = jnp.sum(jnp.where(eye, gam_row[...].reshape(1, CH), 0.0), axis=1, keepdims=True)
+    bet[...] = jnp.sum(jnp.where(eye, bet_row[...].reshape(1, CH), 0.0), axis=1, keepdims=True)
     zc[...] = jnp.zeros_like(zc)
     zn[...] = jnp.zeros_like(zn)
     for b in range(3):
@@ -135,34 +167,6 @@
     cp_xc.wait()
     put_shifts(xcs, 1, xcr[1], xhi)
     put_shifts(xcs, 2, xcr[2], xhi)
-
-    core27 = NZL + (NM - 1) + (NY - 1) + (NX - 1)
-    pl.semaphore_wait(barrier, core27 + has_prev.astype(jnp.int32) + has_next.astype(jnp.int32))
-
-    def halo(src, dst, to_next, i, send, recv):
-        return pltpu.make_async_remote_copy(
-            src_ref=src.at[0, 1] if to_next else src.at[0, 0],
-            dst_ref=dst.at[0] if to_next else dst.at[3],
-            send_sem=send.at[i],
-            recv_sem=recv.at[i],
-            device_id=next_id if to_next else prev_id,
-            device_id_type=pl.DeviceIdType.MESH,
-        )
-
-    halos = (
-        halo(xc_in, xcr, True, 0, hs, hr),
-        halo(xc_in, xcr, False, 1, hs, hr),
-        halo(xn_in, xnr, True, 2, hs, hr),
-        halo(xn_in, xnr, False, 3, hs, hr),
-    )
-
-    @pl.when(has_next)
-    def _():
-        halos[0].start()
-
-    @pl.when(has_prev)
-    def _():
-        halos[1].start()
 
     cp_k.wait()
 
@@ -428,11 +432,10 @@
             device_id={"zl": k, "zh": h}, device_id_type=pl.DeviceIdType.MESH,
         )
 
-    def g_copy(i, slot, t):
-        return pltpu.make_async_remote_copy(
-            src_ref=r6.at[slot], dst_ref=r6.at[slot], send_sem=c6s.at[i], recv_sem=c6r.at[slot],
-            device_id={"x": t}, device_id_type=pl.DeviceIdType.MESH,
-        )
+    forward = pltpu.make_async_remote_copy(
+        src_ref=mine, dst_ref=before, send_sem=fsem.at[0], recv_sem=fsem.at[1],
+        device_id={"x": jnp.minimum(xx + 1, NX - 1)}, device_id_type=pl.DeviceIdType.MESH,
+    )
 
     def summed(k, u):
         return gacc[k, co, u] + r1[k, u].astype(f32)
@@ -494,6 +497,14 @@
     for k in ORDER:
         step_x1(k)
 
+    for step in range(len(ORDER) + 2):
+        if step < 6:
+            step_x2(ORDER[step])
+        if step >= 2:
+            step_y(ORDER[step - 2])
+    for k in ORDER:
+        step_z(k)
+
     @pl.when(has_prev)
     def _():
         gz_next.wait_recv()
@@ -527,27 +538,16 @@
     gx_out[0, 0] = grad_x[:, :COLS]
     gx_out[0, 1] = grad_x[:, COLS:]
 
-    for step in range(len(ORDER) + 5):
-        if step < 6:
-            step_x2(ORDER[step])
-        if 2 <= step < 8:
-            step_y(ORDER[step - 2])
-        if 5 <= step < 11:
-            step_z(ORDER[step - 5])
-
     def gather_z(i, acc):
         t = (z12 + i) % NZ
         z_copy(0, 0, t).wait_recv()
         return acc + r5[t].astype(f32)
 
-    final = lax.fori_loop(1, NZ, gather_z, cown[zl])
-    r6[xx] = final
-
-    def go_x(i, c):
-        g_copy(i, xx, (xx + i) % NX).start()
-        return c
-
-    lax.fori_loop(1, NX, go_x, 0)
+    mine[...] = lax.fori_loop(1, NZ, gather_z, cown[zl])
+
+    @pl.when(xx < NX - 1)
+    def _():
+        forward.start()
 
     @pl.when(has_next)
     def _():
@@ -580,33 +580,42 @@
             def _():
                 z_copy(k, h, z12).wait_send()
 
-    def end_x(i, c):
-        t = (xx + i) % NX
-        g_copy(i, t, t).wait_recv()
-        g_copy(i, xx, t).wait_send()
-        return c
-
-    lax.fori_loop(1, NX, end_x, 0)
-    gk_out[...] = r6[...]
-
-
-def last(y_in, gx_in, raw, y_out, gx_out, gk_out, ybuf, gbuf, rows, sem):
-    pairs = ((y_in, ybuf, y_out), (gx_in, gbuf, gx_out))
-    into = [pltpu.make_async_copy(a, b, sem.at[i]) for i, (a, b, _) in enumerate(pairs)]
-    back = [pltpu.make_async_copy(b, c, sem.at[2 + i]) for i, (_, b, c) in enumerate(pairs)]
-    for cp in into:
+    gk_out[0] = mine[...]
+
+    @pl.when(xx > 0)
+    def _():
+        forward.wait_recv()
+
+    @pl.when(xx == 0)
+    def _():
+        before[...] = jnp.zeros_like(before)
+
+    gk_out[1] = before[...]
+
+    @pl.when(xx < NX - 1)
+    def _():
+        forward.wait_send()
+
+
+def last(y_in, gx_in, raw, y_out, gx_out, gk_out, rows, sem):
+    back = [
+        pltpu.make_async_copy(y_in, y_out, sem.at[0]),
+        pltpu.make_async_copy(gx_in, gx_out, sem.at[1]),
+    ]
+    for cp in back:
         cp.start()
     second, high = lax.axis_index("zh") == 1, lax.axis_index("y") >= NY // 2
-    for u in range(NX):
-        tile = raw[u]
+    for i in range(2):
+        tile = raw[i]
         rest = tile[16:]
         parts = (tile[:8], tile[8:16], jnp.where(high, pltpu.roll(rest, REST, 1), rest))
-        for i, p in enumerate(parts):
-            rows[u * 4 : u * 4 + 4, i * LANES : (i + 1) * LANES] = jnp.where(second, p[4:], p[:4])
-    into[0].wait()
-    back[0].start()
-    into[1].wait()
-    back[1].start()
+        for t, p in enumerate(parts):
+            four = jnp.where(second, p[4:], p[:4])
+            lanes = slice(t * LANES, (t + 1) * LANES)
+            if i == 0:
+                rows[1:5, lanes] = four
+            else:
+                rows[0:1, lanes] = four[3:]
     share = 9 * CH * CH // (NH * NZH * NX)
     for v in range(NX):
 
@@ -615,6 +624,7 @@
             for start in range(0, share, LANES):
                 n = min(LANES, share - start)
                 r, col = divmod(share * v + start, CH)
+                r = r - 4 * v + 1
                 k = min(n, CH - col)
                 piece = rows[r : r + 1, col : col + k]
                 if k < n:
@@ -626,11 +636,12 @@
 
 
 def local(x_next, x_cur, grad_out, kernel, gamma, beta):
-    any_spec = pl.BlockSpec(memory_space=pl.ANY)
     vmem = pl.BlockSpec(memory_space=pltpu.VMEM)
+    hbm = pl.BlockSpec(memory_space=pltpu.HBM)
     dma = pltpu.SemaphoreType.DMA
     V = pltpu.VMEM
     scratch = [
+        V((CH,), f32), V((CH,), f32),
         V((4, CH, COLS), bf16), V((4, CH, COLS), bf16), V((2, CH, COLS), bf16),
         V((3, 3, CH, CH), bf16),
         V((3, 4, CH + REST, COLS), bf16), V((3, 4, 2 * REST, COLS), bf16), V((3, 4, CH, COLS), bf16),
@@ -646,27 +657,27 @@
         V((NZL, NY, 24, LANES), bf16), V((NZL, NY, 24, LANES), bf16),
         V((NZL, NY, 24, LANES), f32),
         V((NZL, 24, LANES), bf16), V((NZL, 24, LANES), f32),
-        V((NZ, 24, LANES), bf16), V((NX, 24, LANES), f32),
-        dma((4,)), dma((4,)), dma((4,)), dma((2,)), dma((2,)),
+        V((NZ, 24, LANES), bf16), V((24, LANES), f32), V((24, LANES), f32),
+        dma((6,)), dma((4,)), dma((4,)), dma((2,)), dma((2,)),
         dma((NM,)), dma((NM,)), dma((NY,)), dma((NY,)),
         dma((NM,)), dma((NM,)), dma((NY,)), dma((NY,)),
         dma((NZL,)), dma((NZL,)), dma((NZL,)), dma((NZL,)), dma((NZL,)), dma((NZL,)),
-        dma((NZL, NY)), dma((NZL, NY)), dma((NZL, NZH)), dma((NZ,)), dma((NX,)), dma((NX,)),
+        dma((NZL, NY)), dma((NZL, NY)), dma((NZL, NZH)), dma((NZ,)), dma((2,)),
     ]
     y_next, grad_x, quarters = pl.pallas_call(
         body,
         out_shape=(
-            jax.ShapeDtypeStruct(x_next.shape, bf16),
-            jax.ShapeDtypeStruct(x_next.shape, bf16),
-            jax.ShapeDtypeStruct((NX, 24, LANES), f32),
+            pltpu.VMEM(x_next.shape, bf16),
+            pltpu.VMEM(x_next.shape, bf16),
+            pltpu.VMEM((2, 24, LANES), f32),
         ),
-        in_specs=[any_spec, any_spec, any_spec, any_spec, vmem, vmem],
+        in_specs=[hbm] * 6,
         out_specs=(vmem, vmem, vmem),
         scratch_shapes=scratch,
         compiler_params=pltpu.CompilerParams(
-            collective_id=0, has_side_effects=True, vmem_limit_bytes=60 * 1024 * 1024
+            collective_id=0, has_side_effects=True, vmem_limit_bytes=40 * 1024 * 1024
         ),
-    )(x_next, x_cur, grad_out, kernel, gamma, beta)
+    )(*(pltpu.with_memory_space_constraint(v, pltpu.HBM) for v in (x_next, x_cur, grad_out, kernel, gamma, beta)))
     return pl.pallas_call(
         last,
         out_shape=(
@@ -674,9 +685,10 @@
             jax.ShapeDtypeStruct(x_next.shape, bf16),
             jax.ShapeDtypeStruct((9 * CH * CH // (NH * NZH * NX),), f32),
         ),
-        in_specs=[any_spec, any_spec, vmem],
-        out_specs=(any_spec, any_spec, vmem),
-        scratch_shapes=[V(x_next.shape, bf16), V(x_next.shape, bf16), V((16, 3 * LANES), f32), dma((4,))],
+        in_specs=[vmem, vmem, vmem],
+        out_specs=(hbm, hbm, vmem),
+        scratch_shapes=[V((8, 3 * LANES), f32), dma((2,))],
+        compiler_params=pltpu.CompilerParams(vmem_limit_bytes=8 * 1024 * 1024),
     )(y_next, grad_x, quarters)
 
 

time: 81 us -> 77.2 us (0.953)
  the two profiles are of different devices: /device:TPU:128 before, /device:TPU:2 now
where the time goes in v3:
time: 77.2 us; the launch traced here: 77.1 us
  Pallas kernels  76.4 us (99%)
    pallas_call x1, Pallas kernels, local(): pl.pallas_call(body, out_shape=(pltpu.VMEM(x_next.shape, bf16), pltpu.VME...  75.1 us

profile of v3, /device:TPU:2, one launch (start us, length us, event | category | flops | bytes accessed | tf_op | source)
XLA Modules:
  0.0 77.1 jit_solution(4080240745589155146)
XLA Ops:
  0.6 75.1 %shard_map.85 = (bf16[1,2,320,128]{3,2,1,0:T(8,128)(2,1)S(1)}, bf16[1,2,320,128]{3,2,1,0:T(8,128)(2,1)S(1)}, f32[2,24,128]{2,1,0:T(8,128)S(1)}) custom-call(bf16[1,2,320,128]{3,2,1,0:T(8,128)(2,1)} %xn_in.1, bf16[1,2,320,128]{3,2,1,0:T(8,128)(2,1)} %xc_in.1, bf16[1,2,320,128]{3,2,1,0:T(8,128)(2,1)} %go_in.1, bf16[3,3,320,320]{3,2,1,0:T(8,128)(2,1)} %k_in.1, ...), custom_call_target="tpu_custom_call" | custom-call | tf_op jit(solution)/shard_map/pallas_call | solution.py:667
  75.7 1.3 %shard_map.86 = (bf16[1,2,320,128]{3,2,1,0:T(8,128)(2,1)}, bf16[1,2,320,128]{3,2,1,0:T(8,128)(2,1)}, f32[1200]{0:T(1024)}) custom-call(bf16[1,2,320,128]{3,2,1,0:T(8,128)(2,1)S(1)} %get-tuple-element.6.y_in, bf16[1,2,320,128]{3,2,1,0:T(8,128)(2,1)S(1)} %get-tuple-element.7.gx_in, f32[2,24,128]{2,1,0:T(8,128)S(1)} %get-tuple-element.8.raw), custom_call_target="tpu_custom_call" | custom-call | tf_op jit(solution)/shard_map/pallas_call | solution.py:681

commit v4 on v3

--- a/solution.py
+++ b/solution.py
@@ -43,9 +43,9 @@
     gam_row, bet_row, xcr, xnr, gor, kv, xcs, xhi, xns, gzo, gzh, gzs,
     zc, zn, nrm, gn, emask, gam, bet, selm,
     ra, rb, ra2, rb2,
-    gacc, s1, r1, s2, r2, s3, r3, s4, r4, bown, s5, cown, r5, mine, before,
+    gacc, s1, r1, s2, r2, s3, r3, s4, r4, bown, s5, cown, r5, zown, s7, r7, mid, s8, r8, mine, before,
     lsem, hs, hr, ghs, ghr, as_, ar, bs, br, as2, ar2, bs2, br2,
-    c1s, c1r, c2s, c2r, c3s, c3r, c4s, c4r, c5s, c5r, fsem,
+    c1s, c1r, c2s, c2r, c3s, c3r, c4s, c4r, c5s, c5r, c7s, c7r, c8s, c8r, fsem,
 ):
     yy, zl, co = lax.axis_index("y"), lax.axis_index("zl"), lax.axis_index("core")
     zh, xx = lax.axis_index("zh"), lax.axis_index("x")
@@ -432,6 +432,18 @@
             device_id={"zl": k, "zh": h}, device_id_type=pl.DeviceIdType.MESH,
         )
 
+    def z_first(k, h, slot):
+        return pltpu.make_async_remote_copy(
+            src_ref=s7.at[k, h], dst_ref=r7.at[slot], send_sem=c7s.at[k, h], recv_sem=c7r.at[slot],
+            device_id={"zl": k, "zh": h}, device_id_type=pl.DeviceIdType.MESH,
+        )
+
+    def y_second(i, slot, t):
+        return pltpu.make_async_remote_copy(
+            src_ref=s8.at[t // 2], dst_ref=r8.at[slot], send_sem=c8s.at[i], recv_sem=c8r.at[slot],
+            device_id={"y": t}, device_id_type=pl.DeviceIdType.MESH,
+        )
+
     forward = pltpu.make_async_remote_copy(
         src_ref=mine, dst_ref=before, send_sem=fsem.at[0], recv_sem=fsem.at[1],
         device_id={"x": jnp.minimum(xx + 1, NX - 1)}, device_id_type=pl.DeviceIdType.MESH,
@@ -454,12 +466,16 @@
     def step_y(k):
         send_x2(k).wait_recv()
         val = summed(k, xx) + r2[k, 0].astype(f32) + r3[k].astype(f32)
-        for i in range(2):
-            bown[k, :, i * 8 : i * 8 + 8, :] = val[i * 64 : i * 64 + 64].reshape(NY, 8, LANES)
+        bown[k, :, :8, :] = val[:64].reshape(NY, 8, LANES)
         rest = val[128:].reshape(NY // 2, 8, LANES)
-        bown[k, : NY // 2, 16:, :] = rest
-        bown[k, NY // 2 :, 16:, :] = rest
+        bown[k, : NY // 2, 8:, :] = rest
+        bown[k, NY // 2 :, 8:, :] = rest
         s4[k] = bown[k].astype(bf16)
+        for t in range(NY):
+            for h in range(NZH):
+                top = 64 + t * 8 + h * 4
+                zown[k, h, t * 4 : t * 4 + 4, :] = val[top : top + 4]
+        s7[k] = zown[k].astype(bf16)
 
         def go(i, c):
             t = (yy + i) % NY
@@ -467,6 +483,36 @@
             return c
 
         lax.fori_loop(1, NY, go, 0)
+        for h in range(NZH):
+
+            @pl.when(jnp.logical_or(zl != k, zh != h))
+            def _():
+                z_first(k, h, z12).start()
+
+    def middle():
+        def take(i, acc):
+            t = (z12 + i) % NZ
+            z_first(0, 0, t).wait_recv()
+            return acc + r7[t].astype(f32)
+
+        val = lax.fori_loop(1, NZ, take, zown[zl, zh]).reshape(NY // 2, 8, LANES)
+        mid[...] = val
+        s8[...] = val.astype(bf16)
+
+        def go(i, c):
+            t = (yy + i) % NY
+            y_second(i, yy, t).start()
+            return c
+
+        lax.fori_loop(1, NY, go, 0)
+
+    def middle_end():
+        def go(i, acc):
+            t = (yy + i) % NY
+            y_second(i, t, t).wait_recv()
+            return acc + r8[t].astype(f32)
+
+        return lax.fori_loop(1, NY, go, mid[yy // 2])
 
     def step_z(k):
         def go(i, acc):
@@ -504,6 +550,7 @@
             step_y(ORDER[step - 2])
     for k in ORDER:
         step_z(k)
+    middle()
 
     @pl.when(has_prev)
     def _():
@@ -543,7 +590,10 @@
         z_copy(0, 0, t).wait_recv()
         return acc + r5[t].astype(f32)
 
-    mine[...] = lax.fori_loop(1, NZ, gather_z, cown[zl])
+    total_z = lax.fori_loop(1, NZ, gather_z, cown[zl])
+    mine[:8] = total_z[:8]
+    mine[8:16] = middle_end()
+    mine[16:] = total_z[8:]
 
     @pl.when(xx < NX - 1)
     def _():
@@ -579,7 +629,13 @@
             @pl.when(jnp.logical_or(zl != k, zh != h))
             def _():
                 z_copy(k, h, z12).wait_send()
-
+                z_first(k, h, z12).wait_send()
+
+    def sent_second(i, c):
+        y_second(i, yy, (yy + i) % NY).wait_send()
+        return c
+
+    lax.fori_loop(1, NY, sent_second, 0)
     gk_out[0] = mine[...]
 
     @pl.when(xx > 0)
@@ -605,12 +661,13 @@
     for cp in back:
         cp.start()
     second, high = lax.axis_index("zh") == 1, lax.axis_index("y") >= NY // 2
+    odd = lax.axis_index("y") % 2 == 1
     for i in range(2):
         tile = raw[i]
         rest = tile[16:]
         parts = (tile[:8], tile[8:16], jnp.where(high, pltpu.roll(rest, REST, 1), rest))
         for t, p in enumerate(parts):
-            four = jnp.where(second, p[4:], p[:4])
+            four = jnp.where(odd if t == 1 else second, p[4:], p[:4])
             lanes = slice(t * LANES, (t + 1) * LANES)
             if i == 0:
                 rows[1:5, lanes] = four
@@ -654,15 +711,19 @@
         V((NZL, NX, TALL, LANES), bf16), V((NZL, NX, TALL, LANES), bf16),
         V((NZL, 2, TALL, LANES), bf16), V((NZL, 2, TALL, LANES), bf16),
         V((NZL, TALL, LANES), bf16), V((NZL, TALL, LANES), bf16),
-        V((NZL, NY, 24, LANES), bf16), V((NZL, NY, 24, LANES), bf16),
-        V((NZL, NY, 24, LANES), f32),
-        V((NZL, 24, LANES), bf16), V((NZL, 24, LANES), f32),
-        V((NZ, 24, LANES), bf16), V((24, LANES), f32), V((24, LANES), f32),
+        V((NZL, NY, 16, LANES), bf16), V((NZL, NY, 16, LANES), bf16),
+        V((NZL, NY, 16, LANES), f32),
+        V((NZL, 16, LANES), bf16), V((NZL, 16, LANES), f32),
+        V((NZ, 16, LANES), bf16),
+        V((NZL, NZH, NY * 4, LANES), f32), V((NZL, NZH, NY * 4, LANES), bf16), V((NZ, NY * 4, LANES), bf16),
+        V((NY // 2, 8, LANES), f32), V((NY // 2, 8, LANES), bf16), V((NY, 8, LANES), bf16),
+        V((24, LANES), f32), V((24, LANES), f32),
         dma((6,)), dma((4,)), dma((4,)), dma((2,)), dma((2,)),
         dma((NM,)), dma((NM,)), dma((NY,)), dma((NY,)),
         dma((NM,)), dma((NM,)), dma((NY,)), dma((NY,)),
         dma((NZL,)), dma((NZL,)), dma((NZL,)), dma((NZL,)), dma((NZL,)), dma((NZL,)),
-        dma((NZL, NY)), dma((NZL, NY)), dma((NZL, NZH)), dma((NZ,)), dma((2,)),
+        dma((NZL, NY)), dma((NZL, NY)), dma((NZL, NZH)), dma((NZ,)),
+        dma((NZL, NZH)), dma((NZ,)), dma((NY,)), dma((NY,)), dma((2,)),
     ]
     y_next, grad_x, quarters = pl.pallas_call(
         body,

time: 77.2 us -> 76.6 us (level)
  the two profiles are of different devices: /device:TPU:2 before, /device:TPU:4 now
where the time goes in v4:
time: 76.6 us; the launch traced here: 76.5 us
  Pallas kernels  75.9 us (99%)
    pallas_call x1, Pallas kernels, local(): pl.pallas_call(body, out_shape=(pltpu.VMEM(x_next.shape, bf16), pltpu.VME...  74.5 us

profile of v4, /device:TPU:4, one launch (start us, length us, event | category | flops | bytes accessed | tf_op | source)
XLA Modules:
  0.0 76.5 jit_solution(15010022883609905489)
XLA Ops:
  0.6 74.5 %shard_map.85 = (bf16[1,2,320,128]{3,2,1,0:T(8,128)(2,1)S(1)}, bf16[1,2,320,128]{3,2,1,0:T(8,128)(2,1)S(1)}, f32[2,24,128]{2,1,0:T(8,128)S(1)}) custom-call(bf16[1,2,320,128]{3,2,1,0:T(8,128)(2,1)} %xn_in.1, bf16[1,2,320,128]{3,2,1,0:T(8,128)(2,1)} %xc_in.1, bf16[1,2,320,128]{3,2,1,0:T(8,128)(2,1)} %go_in.1, bf16[3,3,320,320]{3,2,1,0:T(8,128)(2,1)} %k_in.1, ...), custom_call_target="tpu_custom_call" | custom-call | tf_op jit(solution)/shard_map/pallas_call | solution.py:728
  75.2 1.3 %shard_map.86 = (bf16[1,2,320,128]{3,2,1,0:T(8,128)(2,1)}, bf16[1,2,320,128]{3,2,1,0:T(8,128)(2,1)}, f32[1200]{0:T(1024)}) custom-call(bf16[1,2,320,128]{3,2,1,0:T(8,128)(2,1)S(1)} %get-tuple-element.6.y_in, bf16[1,2,320,128]{3,2,1,0:T(8,128)(2,1)S(1)} %get-tuple-element.7.gx_in, f32[2,24,128]{2,1,0:T(8,128)S(1)} %get-tuple-element.8.raw), custom_call_target="tpu_custom_call" | custom-call | tf_op jit(solution)/shard_map/pallas_call | solution.py:742

commit v5 on v4

--- a/solution.py
+++ b/solution.py
@@ -366,35 +366,45 @@
         else:
             ref[rows, :] = piece
 
+    def blocks(a, b):
+        for d in range(BLOCKS[b]):
+            block = 32 * a + FIRST[b] + d
+            yield d, block // NM, gacc.at[(block // 2) % NZL, block % 2], d == 0 and b > 0
+
     for a in range(3):
         for b in range(3):
-            first = 32 * a + FIRST[b]
-            low = min(max(NH // 2 - first, 0), BLOCKS[b])
             out = dot(picked[b], jnp.concatenate([xcs[b, a, :MAIN], xcs[b, a + 1, :MAIN]], axis=1), NT)
-            rest = []
-            if low > 0:
-                source = jnp.concatenate([xcs[b, a, MAIN:], xcs[b, a + 1, MAIN:]], axis=1)
-                rest.append(dot(picked[b][: low * 32], source, NT))
-            if low < BLOCKS[b]:
-                source = jnp.concatenate([xhi[b, a], xhi[b, a + 1]], axis=1)
-                rest.append(dot(picked[b][low * 32 :], source, NT))
-            for d in range(BLOCKS[b]):
-                block = first + d
-                row = block // NM
-                part, at = (rest[0], d) if d < low else (rest[-1], d - low)
-                again = d == 0 and b > 0
+            for d, row, ref, again in blocks(a, b):
                 for u in range(NX):
-                    ref = gacc.at[(block // 2) % NZL, block % 2, u]
                     top = d * 32 + u * 8
-                    put(ref, slice(row * 8, row * 8 + 8), out[top : top + 8, :LANES], again)
-                    put(ref, slice(64 + row * 8, 72 + row * 8), out[top : top + 8, LANES:], again)
-                    top = at * 32 + u * 8
-                    at_row = 128 + row % 4 * 8
-                    put(ref, slice(at_row, at_row + 8), part[top : top + 8], again or row >= 4)
-
-    def send_core(k):
-        return pltpu.make_async_remote_copy(
-            src_ref=s1.at[k], dst_ref=r1.at[k], send_sem=c1s.at[k], recv_sem=c1r.at[k],
+                    put(ref.at[u], slice(row * 8, row * 8 + 8), out[top : top + 8, :LANES], again)
+                    put(ref.at[u], slice(64 + row * 8, 72 + row * 8), out[top : top + 8, LANES:], again)
+
+    def rest_gradient():
+        for a in range(3):
+            for b in range(3):
+                low = min(max(NH // 2 - 32 * a - FIRST[b], 0), BLOCKS[b])
+                rest = []
+                if low > 0:
+                    source = jnp.concatenate([xcs[b, a, MAIN:], xcs[b, a + 1, MAIN:]], axis=1)
+                    rest.append(dot(picked[b][: low * 32], source, NT))
+                if low < BLOCKS[b]:
+                    source = jnp.concatenate([xhi[b, a], xhi[b, a + 1]], axis=1)
+                    rest.append(dot(picked[b][low * 32 :], source, NT))
+                for d, row, ref, again in blocks(a, b):
+                    part, at = (rest[0], d) if d < low else (rest[-1], d - low)
+                    for u in range(NX):
+                        top = at * 32 + u * 8
+                        at_row = 128 + row % 4 * 8
+                        put(ref.at[u], slice(at_row, at_row + 8), part[top : top + 8], again or row >= 4)
+
+    PARTS = (pl.ds(0, 128), pl.ds(128, 32))
+
+    def send_core(k, part):
+        rows = PARTS[part]
+        return pltpu.make_async_remote_copy(
+            src_ref=s1.at[k, :, rows], dst_ref=r1.at[k, :, rows],
+            send_sem=c1s.at[part, k], recv_sem=c1r.at[part, k],
             device_id={"core": 1 - co}, device_id_type=pl.DeviceIdType.MESH,
         )
 
@@ -408,9 +418,11 @@
         first = partners(k)[0]
         return 3 - first if k < 3 else first + 1 - 2 * (first % 2)
 
-    def send_x1(k):
-        return pltpu.make_async_remote_copy(
-            src_ref=s2.at[k], dst_ref=r2.at[k], send_sem=c2s.at[k], recv_sem=c2r.at[k],
+    def send_x1(k, part):
+        rows = PARTS[part]
+        return pltpu.make_async_remote_copy(
+            src_ref=s2.at[k, :, rows], dst_ref=r2.at[k, :, rows],
+            send_sem=c2s.at[part, k], recv_sem=c2r.at[part, k],
             device_id={"x": partners(k)[0]}, device_id_type=pl.DeviceIdType.MESH,
         )
 
@@ -452,14 +464,21 @@
     def summed(k, u):
         return gacc[k, co, u] + r1[k, u].astype(f32)
 
-    def step_x1(k):
-        send_core(k).wait_recv()
-        s2[k, 0] = summed(k, partners(k)[0]).astype(bf16)
-        s2[k, 1] = summed(k, second_of_first(k)).astype(bf16)
-        send_x1(k).start()
+    def step_core(k, part):
+        rows = PARTS[part]
+        s1[k, :, rows, :] = gacc[k, 1 - co, :, rows, :].astype(bf16)
+        send_core(k, part).start()
+
+    def step_x1(k, part):
+        send_core(k, part).wait_recv()
+        rows = PARTS[part]
+        for i, u in enumerate((partners(k)[0], second_of_first(k))):
+            s2[k, i, rows, :] = (gacc[k, co, u, rows, :] + r1[k, u, rows, :].astype(f32)).astype(bf16)
+        send_x1(k, part).start()
 
     def step_x2(k):
-        send_x1(k).wait_recv()
+        send_x1(k, 0).wait_recv()
+        send_x1(k, 1).wait_recv()
         s3[k] = (summed(k, partners(k)[1]) + r2[k, 1].astype(f32)).astype(bf16)
         send_x2(k).start()
 
@@ -529,19 +548,14 @@
                 z_copy(k, h, z12).start()
 
     for k in ORDER:
-        s1[k] = gacc[k, 1 - co].astype(bf16)
-        send_core(k).start()
-
-    mean_n = column(row2, 2)
-    square_n = column(row2, 3)
-    rstd_n = lax.rsqrt(square_n - mean_n * mean_n + EPS)
-    affine_n = (zn[...] - mean_n) * rstd_n * gam[...] + bet[...]
-    y_next = (affine_n * jax.nn.sigmoid(affine_n)).astype(bf16)
-    y_out[0, 0] = y_next[:, :COLS]
-    y_out[0, 1] = y_next[:, COLS:]
-
+        step_core(k, 0)
     for k in ORDER:
-        step_x1(k)
+        step_x1(k, 0)
+    rest_gradient()
+    for k in ORDER:
+        step_core(k, 1)
+    for k in ORDER:
+        step_x1(k, 1)
 
     for step in range(len(ORDER) + 2):
         if step < 6:
@@ -552,6 +566,14 @@
         step_z(k)
     middle()
 
+    mean_n = column(row2, 2)
+    square_n = column(row2, 3)
+    rstd_n = lax.rsqrt(square_n - mean_n * mean_n + EPS)
+    affine_n = (zn[...] - mean_n) * rstd_n * gam[...] + bet[...]
+    y_next = (affine_n * jax.nn.sigmoid(affine_n)).astype(bf16)
+    y_out[0, 0] = y_next[:, :COLS]
+    y_out[0, 1] = y_next[:, COLS:]
+
     @pl.when(has_prev)
     def _():
         gz_next.wait_recv()
@@ -616,8 +638,9 @@
     sent_all(a_copy, ra2, as2, ar2, m, NM)
     sent_all(b_copy, rb2, bs2, br2, yy, NY)
     for k in range(NZL):
-        send_core(k).wait_send()
-        send_x1(k).wait_send()
+        for part in range(2):
+            send_core(k, part).wait_send()
+            send_x1(k, part).wait_send()
         send_x2(k).wait_send()
 
         def sent_y(i, c):
@@ -721,7 +744,7 @@
         dma((6,)), dma((4,)), dma((4,)), dma((2,)), dma((2,)),
         dma((NM,)), dma((NM,)), dma((NY,)), dma((NY,)),
         dma((NM,)), dma((NM,)), dma((NY,)), dma((NY,)),
-        dma((NZL,)), dma((NZL,)), dma((NZL,)), dma((NZL,)), dma((NZL,)), dma((NZL,)),
+        dma((2, NZL)), dma((2, NZL)), dma((2, NZL)), dma((2, NZL)), dma((NZL,)), dma((NZL,)),
         dma((NZL, NY)), dma((NZL, NY)), dma((NZL, NZH)), dma((NZ,)),
         dma((NZL, NZH)), dma((NZ,)), dma((NY,)), dma((NY,)), dma((2,)),
     ]

time: 76.6 us -> 77.5 us (1.012)
  no operation moved by 1% of the time
where the time goes in v5:
time: 77.5 us; the launch traced here: 77.3 us
  Pallas kernels  76.6 us (99%)
    pallas_call x1, Pallas kernels, local(): pl.pallas_call(body, out_shape=(pltpu.VMEM(x_next.shape, bf16), pltpu.VME...  75.3 us

profile of v5, /device:TPU:4, one launch (start us, length us, event | category | flops | bytes accessed | tf_op | source)
XLA Modules:
  0.0 77.3 jit_solution(16670059500556017808)
XLA Ops:
  0.6 75.3 %shard_map.85 = (bf16[1,2,320,128]{3,2,1,0:T(8,128)(2,1)S(1)}, bf16[1,2,320,128]{3,2,1,0:T(8,128)(2,1)S(1)}, f32[2,24,128]{2,1,0:T(8,128)S(1)}) custom-call(bf16[1,2,320,128]{3,2,1,0:T(8,128)(2,1)} %xn_in.1, bf16[1,2,320,128]{3,2,1,0:T(8,128)(2,1)} %xc_in.1, bf16[1,2,320,128]{3,2,1,0:T(8,128)(2,1)} %go_in.1, bf16[3,3,320,320]{3,2,1,0:T(8,128)(2,1)} %k_in.1, ...), custom_call_target="tpu_custom_call" | custom-call | tf_op jit(solution)/shard_map/pallas_call | solution.py:751
  75.9 1.3 %shard_map.86 = (bf16[1,2,320,128]{3,2,1,0:T(8,128)(2,1)}, bf16[1,2,320,128]{3,2,1,0:T(8,128)(2,1)}, f32[1200]{0:T(1024)}) custom-call(bf16[1,2,320,128]{3,2,1,0:T(8,128)(2,1)S(1)} %get-tuple-element.6.y_in, bf16[1,2,320,128]{3,2,1,0:T(8,128)(2,1)S(1)} %get-tuple-element.7.gx_in, f32[2,24,128]{2,1,0:T(8,128)S(1)} %get-tuple-element.8.raw), custom_call_target="tpu_custom_call" | custom-call | tf_op jit(solution)/shard_map/pallas_call | solution.py:765

commit v6 on v4

--- a/solution.py
+++ b/solution.py
@@ -76,26 +76,26 @@
         greet({"zl": i, "zh": 1 - zh})
         return c
 
-    lax.fori_loop(0, NZL, far_z, 0)
+    lax.fori_loop(0, NZL, far_z, 0, unroll=True)
 
     def far_m(i, c):
         t = (m + i) % NM
         greet({"zl": t // NC, "core": t % NC})
         return c
 
-    lax.fori_loop(1, NM, far_m, 0)
+    lax.fori_loop(1, NM, far_m, 0, unroll=True)
 
     def far_y(i, c):
         greet({"y": (yy + i) % NY})
         return c
 
-    lax.fori_loop(1, NY, far_y, 0)
+    lax.fori_loop(1, NY, far_y, 0, unroll=True)
 
     def far_x(i, c):
         greet({"x": (xx + i) % NX})
         return c
 
-    lax.fori_loop(1, NX, far_x, 0)
+    lax.fori_loop(1, NX, far_x, 0, unroll=True)
 
     cp_xc = pltpu.make_async_copy(xc_in.at[0], xcr.at[pl.ds(1, 2)], lsem.at[0])
     cp_k = pltpu.make_async_copy(k_in, kv, lsem.at[1])
@@ -263,7 +263,7 @@
             copy(buf, send, recv, i, me, (me + i) % n).start()
             return c
 
-        lax.fori_loop(1, n, go, 0)
+        lax.fori_loop(1, n, go, 0, unroll=True)
 
     def wait_all(copy, buf, send, recv, me, n):
         def go(i, c):
@@ -271,7 +271,7 @@
             copy(buf, send, recv, i, t, t).wait_recv()
             return c
 
-        lax.fori_loop(1, n, go, 0)
+        lax.fori_loop(1, n, go, 0, unroll=True)
         return jnp.sum(buf[...], axis=0)
 
     def sent_all(copy, buf, send, recv, me, n):
@@ -482,7 +482,7 @@
             y_copy(k, i, yy, t, t).start()
             return c
 
-        lax.fori_loop(1, NY, go, 0)
+        lax.fori_loop(1, NY, go, 0, unroll=True)
         for h in range(NZH):
 
             @pl.when(jnp.logical_or(zl != k, zh != h))
@@ -495,7 +495,7 @@
             z_first(0, 0, t).wait_recv()
             return acc + r7[t].astype(f32)
 
-        val = lax.fori_loop(1, NZ, take, zown[zl, zh]).reshape(NY // 2, 8, LANES)
+        val = lax.fori_loop(1, NZ, take, zown[zl, zh], unroll=True).reshape(NY // 2, 8, LANES)
         mid[...] = val
         s8[...] = val.astype(bf16)
 
@@ -504,7 +504,7 @@
             y_second(i, yy, t).start()
             return c
 
-        lax.fori_loop(1, NY, go, 0)
+        lax.fori_loop(1, NY, go, 0, unroll=True)
 
     def middle_end():
         def go(i, acc):
@@ -512,7 +512,7 @@
             y_second(i, t, t).wait_recv()
             return acc + r8[t].astype(f32)
 
-        return lax.fori_loop(1, NY, go, mid[yy // 2])
+        return lax.fori_loop(1, NY, go, mid[yy // 2], unroll=True)
 
     def step_z(k):
         def go(i, acc):
@@ -520,7 +520,7 @@
             y_copy(k, i, t, t, t).wait_recv()
             return acc + r4[k, t].astype(f32)
 
-        val = lax.fori_loop(1, NY, go, bown[k, yy])
+        val = lax.fori_loop(1, NY, go, bown[k, yy], unroll=True)
         cown[k] = val
         s5[k] = val.astype(bf16)
         for h in range(NZH):
@@ -590,7 +590,7 @@
         z_copy(0, 0, t).wait_recv()
         return acc + r5[t].astype(f32)
 
-    total_z = lax.fori_loop(1, NZ, gather_z, cown[zl])
+    total_z = lax.fori_loop(1, NZ, gather_z, cown[zl], unroll=True)
     mine[:8] = total_z[:8]
     mine[8:16] = middle_end()
     mine[16:] = total_z[8:]

time: 76.6 us -> 75.8 us (0.990)
  Pallas kernels: 75.9 us -> 75.1 us
    pallas_call x1, Pallas kernels: 74.5 us -> 73.7 us  [local(): pl.pallas_call(body, out_shape=(pltpu.VMEM(x_next.shape, bf16), pltpu.VME...]
where the time goes in v6:
time: 75.8 us; the launch traced here: 75.7 us
  Pallas kernels  75.1 us (99%)
    pallas_call x1, Pallas kernels, local(): pl.pallas_call(body, out_shape=(pltpu.VMEM(x_next.shape, bf16), pltpu.VME...  73.7 us

profile of v6, /device:TPU:4, one launch (start us, length us, event | category | flops | bytes accessed | tf_op | source)
XLA Modules:
  0.0 75.7 jit_solution(8286226675016836816)
XLA Ops:
  0.6 73.7 %shard_map.85 = (bf16[1,2,320,128]{3,2,1,0:T(8,128)(2,1)S(1)}, bf16[1,2,320,128]{3,2,1,0:T(8,128)(2,1)S(1)}, f32[2,24,128]{2,1,0:T(8,128)S(1)}) custom-call(bf16[1,2,320,128]{3,2,1,0:T(8,128)(2,1)} %xn_in.1, bf16[1,2,320,128]{3,2,1,0:T(8,128)(2,1)} %xc_in.1, bf16[1,2,320,128]{3,2,1,0:T(8,128)(2,1)} %go_in.1, bf16[3,3,320,320]{3,2,1,0:T(8,128)(2,1)} %k_in.1, ...), custom_call_target="tpu_custom_call" | custom-call | tf_op jit(solution)/shard_map/pallas_call | solution.py:728
  74.4 1.3 %shard_map.86 = (bf16[1,2,320,128]{3,2,1,0:T(8,128)(2,1)}, bf16[1,2,320,128]{3,2,1,0:T(8,128)(2,1)}, f32[1200]{0:T(1024)}) custom-call(bf16[1,2,320,128]{3,2,1,0:T(8,128)(2,1)S(1)} %get-tuple-element.6.y_in, bf16[1,2,320,128]{3,2,1,0:T(8,128)(2,1)S(1)} %get-tuple-element.7.gx_in, f32[2,24,128]{2,1,0:T(8,128)S(1)} %get-tuple-element.8.raw), custom_call_target="tpu_custom_call" | custom-call | tf_op jit(solution)/shard_map/pallas_call | solution.py:742
